TPU v7x, 32 devices: a whole 2x2x4 slice. The times are simulated.
32 devices in a mesh: fsdp: 8 (over y, x, core), tensor: 4 (over z).
Axes of the slice: x: 2, y: 2, z: 4, core: 2. Of those that a mesh axis runs over, the one named last changes fastest.
Arguments:
- tokens: bfloat16 [16384, 768], P(('fsdp', 'tensor')), may hold values from -6 to 6
- segments: int32 [8, 2048], P('fsdp'), may hold values from 0 to 8, as said below
- query_weight: bfloat16 [768, 768], P('fsdp', 'tensor'), may hold values from -0.21875 to 0.21875
- query_bias: float32 [768], replicated, may hold values from -3 to 3
- key_weight: bfloat16 [768, 768], P('fsdp', 'tensor'), may hold values from -0.21875 to 0.21875
- value_weight: bfloat16 [768, 768], P('fsdp', 'tensor'), may hold values from -0.21875 to 0.21875
- value_bias: float32 [768], replicated, may hold values from -3 to 3
- mix_weight: bfloat16 [768, 768], P('tensor', 'fsdp'), may hold values from -1.75 to 1.75
- mix_bias: float32 [768], replicated, may hold values from -3 to 3
- norm_gain: float32 [768], replicated, may hold values from 0.25 to 1.75
- norm_shift: float32 [768], replicated, may hold values from -3 to 3
- up_weight: bfloat16 [768, 3072], P('fsdp', 'tensor'), may hold values from -0.21875 to 0.21875
- up_bias: float32 [3072], replicated, may hold values from -3 to 3
- down_weight: bfloat16 [3072, 768], P('tensor', 'fsdp'), may hold values from -0.109375 to 0.109375
- down_bias: float32 [768], replicated, may hold values from -3 to 3
- final_gain: float32 [768], replicated, may hold values from 0.25 to 1.75
- final_shift: float32 [768], replicated, may hold values from -3 to 3
- out_grad: bfloat16 [16384, 768], P(('fsdp', 'tensor')), may hold values from -6 to 6
Outputs:
- layer_out: bfloat16 [16384, 768], P(('fsdp', 'tensor'))
- tokens_grad: float32 [16384, 768], P(('fsdp', 'tensor'))
- query_weight_grad: float32 [768, 768], P('fsdp', 'tensor')
- query_bias_grad: float32 [768], replicated
- key_weight_grad: float32 [768, 768], P('fsdp', 'tensor')
- value_weight_grad: float32 [768, 768], P('fsdp', 'tensor')
- value_bias_grad: float32 [768], replicated
- mix_weight_grad: float32 [768, 768], P('tensor', 'fsdp')
- mix_bias_grad: float32 [768], replicated
- norm_gain_grad: float32 [768], replicated
- norm_shift_grad: float32 [768], replicated
- up_weight_grad: float32 [768, 3072], P('fsdp', 'tensor')
- up_bias_grad: float32 [3072], replicated
- down_weight_grad: float32 [3072, 768], P('tensor', 'fsdp')
- down_bias_grad: float32 [768], replicated
- final_gain_grad: float32 [768], replicated
- final_shift_grad: float32 [768], replicated
Inputs may be any that keep to these rules, and one draw needn't show every extreme that they name: `segments`: each row is one sequence: its live part begins at the first position and its ids never decrease along it, running from 1 to 8, with 8 reached in every row and some ids possibly skipped; after it come 1 to 256 padding positions with id 0.
All inputs are finite; a program needn't handle non-finite values.
Results may differ from a plain program's by a relative error of at most 0.013.
The roundings to bfloat16 on the way count: a program that leaves them out, or rounds other values in their place, can miss the bound.
Values may be sent and summed in bfloat16 or wider, within the bound.
No kernel may reach another device: no remote copies, remote signals or barrier semaphores. Data moves between devices by JAX's collectives and lax.ppermute only.
A program may use at most 128 MiB of HBM per device.

v0:
```python
from functools import partial
from functools import reduce

import jax
import jax.numpy as jnp
from jax import lax
from jax.sharding import PartitionSpec as P

HD = 64


EPSILON = 1e-05
MASKED = -1e30


def in_blocks(array, dim, length):
    before, after = (array.shape[:dim], array.shape[dim + 1 :])
    return jnp.moveaxis(array.reshape(*before, length, -1, *after), dim, 0)


def summed_on_arrival(array, axis, dim):
    blocks = in_blocks(array, dim, lax.axis_size(axis))
    arrived = lax.all_to_all(blocks, axis, split_axis=0, concat_axis=0, tiled=True)
    return arrived.astype(jnp.float32).sum(axis=0)


def sent_together(arrays, axis, dim, along):
    ends, at = ([], 0)
    for a in arrays[:-1]:
        at += a.shape[along]
        ends.append(at)
    both = jnp.concatenate(arrays, axis=along)
    return tuple(jnp.split(summed_on_arrival(both, axis, dim), ends, axis=along))


def norm_rows(rows_in, gain_row, shift_row):
    row_mean = jnp.mean(rows_in, axis=-1, keepdims=True)
    centred = rows_in - row_mean
    spread = jnp.mean(centred * centred, axis=-1, keepdims=True)
    return centred * lax.rsqrt(spread + EPSILON) * gain_row + shift_row


def multiply(left_rows, right_matrix, transposed):
    right_dim = 1 if transposed else 0
    return lax.dot_general(
        left_rows,
        right_matrix,
        (((1,), (right_dim,)), ((), ())),
        preferred_element_type=jnp.float32,
    )


def contract_rows(left_rows, right_rows):
    return lax.dot_general(
        left_rows, right_rows, (((0,), (0,)), ((), ())), preferred_element_type=jnp.float32
    )


def gather_rows(local_rows):
    return lax.all_gather(local_rows, "tensor", axis=0, tiled=True)


def reduce_rows(left_list, right_list, transposed, row_count):
    products = [
        multiply(
            lax.slice_in_dim(left_rows, 0, row_count * lax.axis_size("tensor"), axis=0),
            right_matrix,
            transposed,
        )
        for left_rows, right_matrix in zip(left_list, right_list)
    ]
    return lax.psum_scatter(reduce(jnp.add, products), "tensor", scatter_dimension=0, tiled=True)


def attend_forward(query_all, key_all, value_all, segments, query_rows):
    scale = HD ** (-0.5)

    def one_sequence(seq_item):
        query_seq, key_seq, value_seq, seg_seq = seq_item
        blocks = query_seq.shape[0] // query_rows
        query_blocks = query_seq.reshape((blocks, query_rows) + query_seq.shape[1:])
        seg_blocks = seg_seq.reshape(blocks, query_rows)

        def one_block(block_item):
            query_block, seg_block = block_item
            scores = (
                jnp.einsum("qhd,khd->hqk", query_block, key_seq, preferred_element_type=jnp.float32)
                * scale
            )
            same_doc = (seg_block[:, None] == seg_seq[None, :])[None]
            scores = jnp.where(same_doc, scores, MASKED)
            row_max = jnp.max(scores, axis=-1, keepdims=True)
            raised = jnp.exp(scores - row_max)
            row_total = jnp.sum(raised, axis=-1, keepdims=True)
            attn_probs = (raised / row_total).astype(jnp.bfloat16)
            mixed_out = jnp.einsum(
                "hqk,khd->qhd", attn_probs, value_seq, preferred_element_type=jnp.float32
            )
            return (mixed_out, (row_max + jnp.log(row_total))[:, :, 0])

        mixed_out, log_sums = lax.map(one_block, (query_blocks, seg_blocks))
        return (mixed_out.reshape(query_seq.shape), log_sums)

    return lax.map(one_sequence, (query_all, key_all, value_all, segments))


def attend_backward(query_all, key_all, value_all, grad_all, log_all, segments, query_rows):
    scale = HD ** (-0.5)

    def one_sequence(seq_item):
        query_seq, key_seq, value_seq, grad_seq, log_seq, seg_seq = seq_item
        blocks = query_seq.shape[0] // query_rows
        query_blocks = query_seq.reshape((blocks, query_rows) + query_seq.shape[1:])
        grad_blocks = grad_seq.reshape((blocks, query_rows) + grad_seq.shape[1:])
        seg_blocks = seg_seq.reshape(blocks, query_rows)

        def one_block(carried, block_item):
            key_acc, value_acc = carried
            query_block, grad_block, seg_block, log_block = block_item
            scores = (
                jnp.einsum("qhd,khd->hqk", query_block, key_seq, preferred_element_type=jnp.float32)
                * scale
            )
            same_doc = (seg_block[:, None] == seg_seq[None, :])[None]
            scores = jnp.where(same_doc, scores, MASKED)
            attn_probs = jnp.exp(scores - log_block[:, :, None])
            value_acc = value_acc + jnp.einsum(
                "hqk,qhd->khd",
                attn_probs.astype(jnp.bfloat16),
                grad_block,
                preferred_element_type=jnp.float32,
            )
            grad_probs = jnp.einsum(
                "qhd,khd->hqk", grad_block, value_seq, preferred_element_type=jnp.float32
            )
            grad_scores = attn_probs * (
                grad_probs - jnp.sum(attn_probs * grad_probs, axis=-1, keepdims=True)
            )
            score_low = grad_scores.astype(jnp.bfloat16)
            grad_query = (
                jnp.einsum("hqk,khd->qhd", score_low, key_seq, preferred_element_type=jnp.float32)
                * scale
            )
            key_acc = (
                key_acc
                + jnp.einsum(
                    "hqk,qhd->khd", score_low, query_block, preferred_element_type=jnp.float32
                )
                * scale
            )
            return ((key_acc, value_acc), grad_query)

        zeros_keys = jnp.zeros(key_seq.shape, jnp.float32)
        (grad_key, grad_value), grad_query = lax.scan(
            one_block, (zeros_keys, zeros_keys), (query_blocks, grad_blocks, seg_blocks, log_seq)
        )
        return (grad_query.reshape(query_seq.shape), grad_key, grad_value)

    return lax.map(one_sequence, (query_all, key_all, value_all, grad_all, log_all, segments))


def on_device(
    tokens,
    segments,
    query_weight,
    query_bias,
    key_weight,
    value_weight,
    value_bias,
    mix_weight,
    mix_bias,
    norm_gain,
    norm_shift,
    up_weight,
    up_bias,
    down_weight,
    down_bias,
    final_gain,
    final_shift,
    out_grad,
):
    tensor_rank = lax.axis_index("tensor")
    head_width = query_weight.shape[1]
    unit_width = up_weight.shape[1]
    local_count = tokens.shape[0]
    seq_count = segments.shape[0]
    seq_length = segments.shape[1]
    heads_local = head_width // HD
    query_rows = min(512, seq_length)
    head_shape = (seq_count, seq_length, heads_local, HD)
    query_full, key_full, value_full, mix_full = (
        lax.all_gather(query_weight, "fsdp", axis=0, tiled=True),
        lax.all_gather(key_weight, "fsdp", axis=0, tiled=True),
        lax.all_gather(value_weight, "fsdp", axis=0, tiled=True),
        lax.all_gather(mix_weight, "fsdp", axis=1, tiled=True),
    )
    up_full, down_full = (
        lax.all_gather(up_weight, "fsdp", axis=0, tiled=True),
        lax.all_gather(down_weight, "fsdp", axis=1, tiled=True),
    )
    query_shift = lax.dynamic_slice_in_dim(query_bias, tensor_rank * head_width, head_width)
    value_shift = lax.dynamic_slice_in_dim(value_bias, tensor_rank * head_width, head_width)
    unit_shift = lax.dynamic_slice_in_dim(up_bias, tensor_rank * unit_width, unit_width)
    tokens_all = gather_rows(tokens)
    query_low = (multiply(tokens_all, query_full, False) + query_shift).astype(jnp.bfloat16)
    key_low = multiply(tokens_all, key_full, False).astype(jnp.bfloat16)
    value_low = (multiply(tokens_all, value_full, False) + value_shift).astype(jnp.bfloat16)
    mixed_out, log_sums = attend_forward(
        query_low.reshape(head_shape),
        key_low.reshape(head_shape),
        value_low.reshape(head_shape),
        segments,
        query_rows,
    )
    context_low = mixed_out.reshape(-1, head_width).astype(jnp.bfloat16)
    attn_local = reduce_rows([context_low], [mix_full], False, local_count)
    first_sum = tokens.astype(jnp.float32) + attn_local + mix_bias
    normed, first_pull = jax.vjp(norm_rows, first_sum, norm_gain, norm_shift)
    normed_low = normed.astype(jnp.bfloat16)
    normed_all = gather_rows(normed_low)
    pre_act = multiply(normed_all, up_full, False) + unit_shift
    gelu_tanh = partial(jax.nn.gelu, approximate=True)
    activated, gelu_pull = jax.vjp(gelu_tanh, pre_act)
    act_low = activated.astype(jnp.bfloat16)
    ffn_local = reduce_rows([act_low], [down_full], False, local_count)
    second_sum = normed + ffn_local + down_bias
    layer_value, final_pull = jax.vjp(norm_rows, second_sum, final_gain, final_shift)
    layer_out = layer_value.astype(jnp.bfloat16)
    own_segments = lax.dynamic_slice_in_dim(
        segments.reshape(-1), tensor_rank * local_count, local_count
    )
    live_rows = (own_segments > 0).astype(jnp.float32)[:, None]
    grad_second, grad_final_gain, grad_final_shift = final_pull(
        out_grad.astype(jnp.float32) * live_rows
    )
    up_back, down_back = (
        lax.all_gather(up_weight, "fsdp", axis=0, tiled=True),
        lax.all_gather(down_weight, "fsdp", axis=1, tiled=True),
    )
    second_low = grad_second.astype(jnp.bfloat16)
    second_all = gather_rows(second_low)
    grad_down = contract_rows(act_low, second_all)
    grad_act = multiply(second_all, down_back, True)
    grad_pre = gelu_pull(grad_act)[0].astype(jnp.bfloat16)
    grad_up = contract_rows(normed_all, grad_pre)
    up_weight_grad, down_weight_grad = (
        lax.psum_scatter(grad_up, "fsdp", scatter_dimension=0, tiled=True),
        lax.psum_scatter(grad_down, "fsdp", scatter_dimension=1, tiled=True),
    )
    grad_normed = grad_second + reduce_rows([grad_pre], [up_back], True, local_count)
    grad_first, grad_norm_gain, grad_norm_shift = first_pull(grad_normed)
    query_back, key_back, value_back, mix_back = (
        lax.all_gather(query_weight, "fsdp", axis=0, tiled=True),
        lax.all_gather(key_weight, "fsdp", axis=0, tiled=True),
        lax.all_gather(value_weight, "fsdp", axis=0, tiled=True),
        lax.all_gather(mix_weight, "fsdp", axis=1, tiled=True),
    )
    first_low = grad_first.astype(jnp.bfloat16)
    first_all = gather_rows(first_low)
    grad_mix = contract_rows(context_low, first_all)
    grad_context = multiply(first_all, mix_back, True).astype(jnp.bfloat16)
    grad_query, grad_key, grad_value = attend_backward(
        query_low.reshape(head_shape),
        key_low.reshape(head_shape),
        value_low.reshape(head_shape),
        grad_context.reshape(head_shape),
        log_sums,
        segments,
        query_rows,
    )
    query_grad_low = grad_query.reshape(-1, head_width).astype(jnp.bfloat16)
    key_grad_low = grad_key.reshape(-1, head_width).astype(jnp.bfloat16)
    value_grad_low = grad_value.reshape(-1, head_width).astype(jnp.bfloat16)
    tokens_grad = grad_first + reduce_rows(
        [query_grad_low, key_grad_low, value_grad_low],
        [query_back, key_back, value_back],
        True,
        local_count,
    )
    grad_query_w = contract_rows(tokens_all, query_grad_low)
    grad_key_w = contract_rows(tokens_all, key_grad_low)
    grad_value_w = contract_rows(tokens_all, value_grad_low)
    query_weight_grad, key_weight_grad, value_weight_grad, mix_weight_grad = (
        *sent_together(
            (
                grad_query_w.astype(jnp.bfloat16),
                grad_key_w.astype(jnp.bfloat16),
                grad_value_w.astype(jnp.bfloat16),
            ),
            "fsdp",
            0,
            1,
        ),
        summed_on_arrival(grad_mix.astype(jnp.bfloat16), "fsdp", 1),
    )
    zeros_model = jnp.zeros(query_bias.shape, jnp.float32)
    query_bias_part = lax.dynamic_update_slice_in_dim(
        zeros_model, jnp.sum(query_grad_low, axis=0, dtype=jnp.float32), tensor_rank * head_width, 0
    )
    value_bias_part = lax.dynamic_update_slice_in_dim(
        zeros_model, jnp.sum(value_grad_low, axis=0, dtype=jnp.float32), tensor_rank * head_width, 0
    )
    up_bias_part = lax.dynamic_update_slice_in_dim(
        jnp.zeros(up_bias.shape, jnp.float32),
        jnp.sum(grad_pre, axis=0, dtype=jnp.float32),
        tensor_rank * unit_width,
        0,
    )
    small_sums = lax.psum(
        (
            query_bias_part,
            value_bias_part,
            jnp.sum(grad_first, axis=0),
            grad_norm_gain,
            grad_norm_shift,
            up_bias_part,
            jnp.sum(grad_second, axis=0),
            grad_final_gain,
            grad_final_shift,
        ),
        ("fsdp", "tensor"),
    )
    return (
        layer_out,
        tokens_grad,
        query_weight_grad,
        small_sums[0],
        key_weight_grad,
        value_weight_grad,
        small_sums[1],
        mix_weight_grad,
        small_sums[2],
        small_sums[3],
        small_sums[4],
        up_weight_grad,
        small_sums[5],
        down_weight_grad,
        small_sums[6],
        small_sums[7],
        small_sums[8],
    )


def solution(mesh):
    placed = (
        P(("fsdp", "tensor"), None),
        P("fsdp", None),
        P("fsdp", "tensor"),
        P(),
        P("fsdp", "tensor"),
        P("fsdp", "tensor"),
        P(),
        P("tensor", "fsdp"),
        P(),
        P(),
        P(),
        P("fsdp", "tensor"),
        P(),
        P("tensor", "fsdp"),
        P(),
        P(),
        P(),
        P(("fsdp", "tensor"), None),
    )
    return jax.shard_map(
        on_device,
        mesh=mesh,
        in_specs=placed,
        out_specs=(
            P(("fsdp", "tensor"), None),
            P(("fsdp", "tensor"), None),
            P("fsdp", "tensor"),
            P(),
            P("fsdp", "tensor"),
            P("fsdp", "tensor"),
            P(),
            P("tensor", "fsdp"),
            P(),
            P(),
            P(),
            P("fsdp", "tensor"),
            P(),
            P("tensor", "fsdp"),
            P(),
            P(),
            P(),
        ),
        check_vma=False,
    )
```

profile of v0, /device:TPU:0, one launch (start us, length us, event | category | flops | bytes accessed | tf_op | source)
XLA Modules:
  0.0 1114.1 jit_solution(8420585453225565310)
XLA Ops:
  13.7 11.0 all_gather.40
  24.7 9.5 all_gather.37
  34.3 8.8 all_gather.38
  43.1 9.5 all_gather.39
  52.6 24.1 %all-gather.7.cloned.1.call-done = bf16[2048,768]{1,0:T(8,128)(2,1)} async-done(((bf16[512,768]{1,0:T(8,128)(2,1)}), bf16[2048,768]{1,0:T(8,128)(2,1)}) %all-gather.7.cloned.1.call-update) | async-done | bytes 3145744 | tf_op jit(solution)/shard_map/all_gather | solution.py:60
  85.1 82.9 %while.47 = (s32[]{:T(128)}, bf16[4,512,3,64]{1,3,2,0:T(8,128)(2,1)S(1)}, f32[4,3,512]{2,1,0:T(4,128)}, s32[4,512]{1,0:T(4,128)S(1)}, s32[2048]{0:T(1024)S(1)}, ...) while((s32[]{:T(128)}, ...), condition=%wide.region_3.4_spmd, body=%wide.region_0.3_spmd.sunk | while | flops 844102144 | bytes 44175476 | solution.py:101
  85.7 6.0 fusion.134
  91.7 6.8 fusion.135
  98.5 6.7 fusion.136
  106.5 6.0 fusion.134
  112.4 6.8 fusion.135
  119.2 6.7 fusion.136
  127.2 6.0 fusion.134
  133.2 6.8 fusion.135
  139.9 6.7 fusion.136
  147.9 6.0 fusion.134
  153.9 6.8 fusion.135
  160.7 6.7 fusion.136
  174.1 108.9 %reduce-scatter.7.cloned.1.call-done = f32[512,768]{1,0:T(8,128)} async-done(((f32[2048,768]{1,0:T(8,128)}), f32[512,768]{1,0:T(8,128)}) %reduce-scatter.7.cloned.1.call-update) | async-done | bytes 1572880 | tf_op jit(solution)/shard_map/reduce_scatter | solution.py:72
  290.8 61.6 %all-gather.9.cloned.1.call-done = bf16[2048,768]{1,0:T(8,128)(2,1)} async-done(((bf16[512,768]{1,0:T(8,128)(2,1)}), bf16[2048,768]{1,0:T(8,128)(2,1)}) %all-gather.9.cloned.1.call-update) | async-done | bytes 3145744 | tf_op jit(solution)/shard_map/all_gather | solution.py:60
  352.3 9.7 multiply_convert_fusion.1
  362.0 14.6 %all-gather.13.cloned.1.call-done = bf16[768,768]{0,1:T(8,128)(2,1)} async-done(((bf16[768,96]{0,1:T(8,128)(2,1)}), bf16[768,768]{0,1:T(8,128)(2,1)}) %all-gather.13.cloned.1.call-update) | async-done | bytes 1179664 | tf_op jit(solution)/shard_map/all_gather | solution.py:199
  376.6 7.5 fusion.65
  384.8 110.1 %reduce-scatter.9.cloned.1.call-done = f32[512,768]{1,0:T(8,128)} async-done(((f32[2048,768]{1,0:T(8,128)}), f32[512,768]{1,0:T(8,128)}) %reduce-scatter.9.cloned.1.call-update) | async-done | bytes 1572880 | tf_op jit(solution)/shard_map/reduce_scatter | solution.py:72
  503.3 64.1 %all-gather.15.cloned.1.call-done = bf16[2048,768]{1,0:T(8,128)(2,1)} async-done(((bf16[512,768]{1,0:T(8,128)(2,1)}), bf16[2048,768]{1,0:T(8,128)(2,1)}) %all-gather.15.cloned.1.call-update) | async-done | bytes 3145744 | tf_op jit(solution)/shard_map/all_gather | solution.py:60
  567.4 9.4 convert_reduce_fusion
  583.1 109.4 %reduce-scatter.11.cloned.1.call-done = f32[512,768]{1,0:T(8,128)} async-done(((f32[2048,768]{1,0:T(8,128)}), f32[512,768]{1,0:T(8,128)}) %reduce-scatter.11.cloned.1.call-update) | async-done | bytes 1572880 | tf_op jit(solution)/shard_map/reduce_scatter | solution.py:72
  699.6 64.1 %all-gather.17.cloned.1.call-done = bf16[2048,768]{1,0:T(8,128)(2,1)} async-done(((bf16[512,768]{1,0:T(8,128)(2,1)}), bf16[2048,768]{1,0:T(8,128)(2,1)}) %all-gather.17.cloned.1.call-update) | async-done | bytes 3145744 | tf_op jit(solution)/shard_map/all_gather | solution.py:60
  768.4 121.8 %while.48 = (s32[]{:T(128)}, f32[2048,3,64]{0,2,1:T(8,128)}, f32[2048,3,64]{0,2,1:T(8,128)}, bf16[4,512,3,64]{1,3,2,0:T(8,128)(2,1)}, bf16[4,512,3,64]{1,3,2,0:T...) while((s32[]{:T(128)}, f32[2048,3,64]{0,2,1:T(8,128)}, ...), condition=%wide.region_17.18_spmd.clone, body=%wide.region_15.17_spmd.clone.sunk | while | flops 2063563264 | bytes 156690832 | solution.py:154
  776.6 5.8 multiply_reduce_fusion.8
  782.4 6.1 multiply_convert_fusion.3
  788.5 5.8 fusion.149
  800.1 6.1 fusion.148
  806.2 5.8 multiply_reduce_fusion.8
  812.0 6.1 multiply_convert_fusion.3
  818.1 5.8 fusion.149
  831.2 6.1 fusion.148
  843.0 6.1 multiply_convert_fusion.3
  849.1 5.8 fusion.149
  862.2 6.1 fusion.148
  874.1 6.1 multiply_convert_fusion.3
  880.2 5.8 fusion.149
  903.9 6.0 fusion.69
  909.9 6.9 fusion.70
  940.3 54.4 %all-reduce = (f32[768]{0:T(1024)}, f32[768]{0:T(1024)}, f32[768]{0:T(1024)}, f32[768]{0:T(1024)}, f32[768]{0:T(1024)}, /*index=5*/f32[3072]{0:T(1024)}, f32[768]{0:T(1024)}, f32[768]{0:T(1024)}, f32[768]{0:T(1024)}) all-reduce(f32[768]{0:T(1024)S(1)} %dynamic_update_slice.32, ...), channel_id=1, replica_groups=mesh['fsdp'=8,'tensor'=4] {'fsdp','tensor'}, use_global_device_ids=true, to_apply=%region_21.22 | all-reduce | flops 9216 | bytes 73728 | tf_op jit(solution)/shard_map/psum | solution.py:309
  997.3 15.4 %reduce-scatter.13.cloned.1.call-done = f32[512,768]{1,0:T(8,128)} async-done(((f32[2048,768]{1,0:T(8,128)}), f32[512,768]{1,0:T(8,128)}) %reduce-scatter.13.cloned.1.call-update) | async-done | bytes 1572880 | tf_op jit(solution)/shard_map/reduce_scatter | solution.py:72
  1015.4 44.0 %reduce-scatter.15.cloned.1.call-done = f32[96,768]{1,0:T(8,128)} async-done(((f32[768,768]{1,0:T(8,128)}), f32[96,768]{1,0:T(8,128)}) %reduce-scatter.15.cloned.1.call-update) | async-done | bytes 294928 | tf_op jit(solution)/shard_map/reduce_scatter | solution.py:247
  1059.5 46.8 %reduce-scatter.17.cloned.1.call-done = f32[768,96]{0,1:T(8,128)} async-done(((f32[768,768]{0,1:T(8,128)}), f32[768,96]{0,1:T(8,128)}) %reduce-scatter.17.cloned.1.call-update) | async-done | bytes 294928 | tf_op jit(solution)/shard_map/reduce_scatter | solution.py:248
  (290 shorter events, 145.6 us)
Async XLA Ops:
  8.0 68.6 %all-gather.7.cloned.1.call-start = ((), (), s32[]{:S(2)}) async-start(), calls=%async_computation.8 | async-start | bytes 3932160 | tf_op jit(solution)/shard_map/all_gather | solution.py:60
  8.8 274.3 %reduce-scatter.7.cloned.1.call-start = ((), (), s32[]{:S(2)}) async-start(), calls=%async_computation.9 | async-start | bytes 7864320 | tf_op jit(solution)/shard_map/reduce_scatter | solution.py:72
  34.3 42.4 %copy-start.24 = (bf16[768,192]{1,0:T(8,128)(2,1)}, bf16[768,192]{1,0:T(8,128)(2,1)S(1)}, u32[]{:S(2)}) copy-start(bf16[768,192]{1,0:T(8,128)(2,1)S(1)} %all_gather.37) | copy-start | bytes 884740
  43.1 37.4 %copy-start.21 = (bf16[768,192]{1,0:T(8,128)(2,1)}, bf16[768,192]{1,0:T(8,128)(2,1)S(1)}, u32[]{:S(2)}) copy-start(bf16[768,192]{1,0:T(8,128)(2,1)S(1)} %all_gather.38) | copy-start | bytes 884740
  52.6 31.1 %copy-start.26 = (bf16[768,192]{1,0:T(8,128)(2,1)}, bf16[768,192]{1,0:T(8,128)(2,1)S(1)}, u32[]{:S(2)}) copy-start(bf16[768,192]{1,0:T(8,128)(2,1)S(1)} %all_gather.39) | copy-start | bytes 884740
  168.0 5.5 copy-start.6
  173.5 117.3 %all-gather.11.cloned.1.call-start = ((), (), s32[]{:S(2)}) async-start(), calls=%async_computation.11 | async-start | bytes 1327104 | tf_op jit(solution)/shard_map/all_gather | solution.py:198
  174.1 178.3 %all-gather.9.cloned.1.call-start = ((), (), s32[]{:S(2)}) async-start(), calls=%async_computation.10 | async-start | bytes 3932160 | tf_op jit(solution)/shard_map/all_gather | solution.py:60
  288.4 88.3 %all-gather.13.cloned.1.call-start = ((), (), s32[]{:S(2)}) async-start(), calls=%async_computation.12 | async-start | bytes 1327104 | tf_op jit(solution)/shard_map/all_gather | solution.py:199
  288.9 206.0 %reduce-scatter.9.cloned.1.call-start = ((), (), s32[]{:S(2)}) async-start(), calls=%async_computation.13 | async-start | bytes 7864320 | tf_op jit(solution)/shard_map/reduce_scatter | solution.py:72
  384.2 183.3 %all-gather.15.cloned.1.call-start = ((), (), s32[]{:S(2)}) async-start(), calls=%async_computation.14 | async-start | bytes 3932160 | tf_op jit(solution)/shard_map/all_gather | solution.py:60
  503.3 189.2 %reduce-scatter.11.cloned.1.call-start = ((), (), s32[]{:S(2)}) async-start(), calls=%async_computation.15 | async-start | bytes 7864320 | tf_op jit(solution)/shard_map/reduce_scatter | solution.py:72
  567.4 11.0 copy-start.51
  583.0 180.6 %all-gather.17.cloned.1.call-start = ((), (), s32[]{:S(2)}) async-start(), calls=%async_computation.16 | async-start | bytes 3932160 | tf_op jit(solution)/shard_map/all_gather | solution.py:60
  692.4 3.5 copy-start.31
  692.4 3.5 copy-start.33
  699.5 313.2 %reduce-scatter.13.cloned.1.call-start = ((), (), s32[]{:S(2)}) async-start(), calls=%async_computation.17 | async-start | bytes 7864320 | tf_op jit(solution)/shard_map/reduce_scatter | solution.py:72
  788.5 5.8 copy-start
  788.5 5.8 copy-start.15
  818.0 5.8 copy-start
  818.0 5.8 copy-start.15
  823.9 4.0 copy-start.3
  823.9 4.0 copy-start.20
  849.1 5.8 copy-start
  849.1 5.8 copy-start.15
  854.9 4.0 copy-start.3
  854.9 4.0 copy-start.20
  880.2 5.8 copy-start
  880.2 5.8 copy-start.15
  886.0 4.0 copy-start.3
  886.0 4.0 copy-start.20
  891.7 5.2 copy-start.12
  891.7 4.1 copy-start.22
  902.0 157.4 %reduce-scatter.15.cloned.1.call-start = ((), (), s32[]{:S(2)}) async-start(), calls=%async_computation.18 | async-start | bytes 2654208 | tf_op jit(solution)/shard_map/reduce_scatter | solution.py:247
  909.9 196.4 %reduce-scatter.17.cloned.1.call-start = ((), (), s32[]{:S(2)}) async-start(), calls=%async_computation.19 | async-start | bytes 2654208 | tf_op jit(solution)/shard_map/reduce_scatter | solution.py:248
  916.9 10.4 copy-start.5
  922.9 12.7 %all-to-all-start.1 = ((bf16[8,192,96]{2,1,0:T(8,128)(2,1)}), bf16[8,192,96]{2,1,0:T(8,128)(2,1)}, u32[]{:S(2)}, u32[]{:S(2)}) async-start(bf16[8,192,96]{2,1,0:T(8,128)(2,1)} %bitcast.115), calls=%async_computation.5 | async-start | bytes 786432 | tf_op jit(solution)/shard_map/all_to_all | solution.py:23
  931.2 8.0 copy-start.47
  931.2 8.3 copy-start.18
  931.2 9.0 copy-start.40
  931.3 9.0 copy-start.41
  931.3 9.0 copy-start.42
  931.3 9.0 copy-start.43
  931.3 9.0 copy-start.45
  931.3 9.0 copy-start.46
  931.4 81.3 %copy-start.8 = (f32[512,768]{1,0:T(8,128)S(1)}, f32[512,768]{1,0:T(8,128)}, u32[]{:S(2)}) copy-start(f32[512,768]{1,0:T(8,128)} %copy-done.7) | copy-start | bytes 4718596
  931.4 81.3 %copy-start.38 = (f32[512]{0:T(512)S(1)}, f32[512]{0:T(512)}, u32[]{:S(2)}) copy-start(f32[512]{0:T(512)} %copy-done.37) | copy-start | bytes 6148
  935.6 60.8 %all-to-all-start = ((bf16[8,96,576]{2,1,0:T(8,128)(2,1)}), bf16[8,96,576]{2,1,0:T(8,128)(2,1)S(1)}, u32[]{:S(2)}, u32[]{:S(2)}) async-start(bf16[8,96,576]{2,1,0:T(8,128)(2,1)} %bitcast.14), calls=%async_computation.4 | async-start | bytes 1966080 | tf_op jit(solution)/shard_map/all_to_all | solution.py:23
  (43 other events, 101.4 us)
Sparse Core Ops, SparseCore 0:
  10.4 66.1 all-gather.6
  173.6 109.3 reduce-scatter.6
  503.4 64.0 all-gather.14
  699.6 64.0 all-gather.16
  902.2 110.4 reduce-scatter.12
  1016.4 42.9 reduce-scatter.14
  1063.8 42.4 reduce-scatter.16
Sparse Core Ops, SparseCore 1:
  175.8 22.5 all-gather.10
  288.4 63.8 all-gather.8
  354.1 22.5 all-gather.12
  384.2 110.6 reduce-scatter.8
  583.1 109.3 reduce-scatter.10
where the time goes:
time: 1120 us; the launch traced here: 1110 us
  waiting for transfers between devices  668 us (60%)
  matrix products  213 us (19%)
  blocking collectives  93.3 us (8%)
  other arithmetic  86.2 us (8%)
  local copies, waits for them, and re-layouts  27.2 us (2%)
  between operations  16.7 us (1%)
    reduce_scatter x4, waiting for transfers between devices, reduce_rows(): lax.psum_scatter(reduce(jnp.add, products), 'tensor', scatter_dimension=0...  344 us
    all_gather x4, waiting for transfers between devices, gather_rows(): return lax.all_gather(local_rows, 'tensor', axis=0, tiled=True)  214 us
    psum x1, blocking collectives, on_device(): lax.psum((query_bias_part, value_bias_part, jnp.sum(grad_first, axis=0),...  54.4 us
    dot_general x12, matrix products, multiply(): lax.dot_general(left_rows, right_matrix, (((1,), (right_dim,)), ((), ()))...  51.3 us
    reduce_scatter x1, waiting for transfers between devices, on_device(): lax.psum_scatter(grad_down, 'fsdp', scatter_dimension=1, tiled=True)  46.8 us
    reduce_scatter x1, waiting for transfers between devices, on_device(): lax.psum_scatter(grad_up, 'fsdp', scatter_dimension=0, tiled=True)  44 us
    dot_general x8, matrix products, one_block(): jnp.einsum('qhd,khd->hqk', query_block, key_seq, preferred_element_type=j...  31.3 us
    reduce_sum x4, other arithmetic, one_block(): row_total = jnp.sum(raised, axis=-1, keepdims=True)  27.1 us
  transfers between devices with their start and end apart: 14, of which 12 were waited for; matrix products, arithmetic and copies ran while one was open for 5% of the time, Pallas kernels for 0%

commit v1 on v0

v1 whole, which is shorter than its diff:
```python
from functools import partial

import jax
import jax.numpy as jnp
from jax import lax
from jax.experimental import pallas as pl
from jax.experimental.pallas import tpu as pltpu
from jax.sharding import PartitionSpec as P

HD = 64
LANES = 128
EPSILON = 1e-05
MASKED = -1e30
BLOCK = 256
LOG2E = 1.4426950408889634
BF = jnp.bfloat16
F32 = jnp.float32


def gather_line(own):
    t = lax.axis_index("tensor")
    below = lax.ppermute(own, "tensor", [(0, 1), (1, 2), (2, 3)])
    above = lax.ppermute(own, "tensor", [(1, 0), (2, 1), (3, 2)])
    slot_a = jnp.where(t < 3, above, below)
    below2 = lax.ppermute(below, "tensor", [(1, 2), (2, 3)])
    above2 = lax.ppermute(above, "tensor", [(2, 1), (1, 0)])
    slot_c = jnp.where(t < 2, above2, below2)
    far = lax.ppermute(slot_c, "tensor", [(1, 0), (2, 3)])
    slot_b = jnp.where((t == 0) | (t == 3), far, below)
    return own, slot_a, slot_c, slot_b


def slot_owner(t):
    return (
        t,
        jnp.where(t < 3, t + 1, 2),
        lax.rem(t + 2, 4),
        jnp.where(t == 3, 0, lax.rem(t + 3, 4)),
    )


def line_order(slots):
    t = lax.axis_index("tensor")
    own, a, c, b = slots

    def pick(v0, v1, v2, v3):
        return jnp.where(t == 0, v0, jnp.where(t == 1, v1, jnp.where(t == 2, v2, v3)))

    return [
        pick(own, b, c, b),
        pick(a, own, b, c),
        pick(c, a, own, a),
        pick(b, c, a, own),
    ]


def reduce_line(part):
    t = lax.axis_index("tensor")
    ends = [(0, 1), (3, 2)]
    b, c, a, own = part("B"), part("C"), part("A"), part("own")
    r1 = lax.ppermute(b.astype(BF), "tensor", ends).astype(F32)
    c = (c.astype(F32) + r1).astype(BF)
    rx = lax.ppermute(c, "tensor", ends).astype(F32)
    ry = lax.ppermute(c, "tensor", [(1, 2), (2, 1)]).astype(F32)
    up = (a.astype(F32) + jnp.where(t == 1, rx, ry)).astype(BF)
    down = jnp.where(t == 3, a.astype(F32), b.astype(F32) + jnp.where(t == 1, ry, rx)).astype(BF)
    from_below = lax.ppermute(up, "tensor", [(0, 1), (1, 2), (2, 3)])
    from_above = lax.ppermute(down, "tensor", [(1, 0), (2, 1), (3, 2)])
    return own.astype(F32) + from_below.astype(F32) + from_above.astype(F32)


def partner(bit):
    n = lax.axis_size("fsdp")
    return [(i, i ^ bit) for i in range(n)]


def fsdp_bits():
    n = lax.axis_size("fsdp")
    bits = [1 << k for k in range(n.bit_length() - 1)]
    return bits


def grow(block, bit):
    f = lax.axis_index("fsdp")
    other = lax.ppermute(block, "fsdp", partner(bit))
    high = (f & bit) != 0
    return jnp.stack([jnp.where(high, other, block), jnp.where(high, block, other)])


def gather_fsdp(block):
    n = lax.axis_size("fsdp")
    bits = fsdp_bits()
    m, r, c = block.shape
    half = m // 2
    outer = bits[1:]
    pieces = []
    for rows, order in ((block[:half], outer), (block[half:], outer[::-1])):
        done = []
        for bit in order:
            rows = grow(rows, bit)
            done.insert(0, bit)
        rows = grow(rows, bits[0])
        done.insert(0, bits[0])
        k = len(done)
        want = sorted(done, reverse=True)
        axes = [k] + [done.index(b) for b in want] + [k + 1, k + 2]
        pieces.append(rows.transpose(axes).reshape(half, n * r, c))
    return jnp.concatenate(pieces, axis=0)


def halve(block, axis, bit):
    f = lax.axis_index("fsdp")
    mine = jnp.where((f & bit) != 0, 1, 0)
    keep = lax.dynamic_index_in_dim(block, mine, axis, keepdims=False)
    send = lax.dynamic_index_in_dim(block, 1 - mine, axis, keepdims=False)
    got = lax.ppermute(send, "fsdp", partner(bit))
    return (keep.astype(F32) + got.astype(F32)).astype(BF)


def reduce_fsdp(block):
    n = lax.axis_size("fsdp")
    bits = fsdp_bits()
    k = len(bits)
    m, rows, c = block.shape
    block = block.reshape((m,) + (2,) * k + (rows // n, c))
    block = halve(block, k, bits[0])
    half = m // 2
    pieces = []
    for part, order in ((block[:half], bits[1:]), (block[half:], bits[:0:-1])):
        left = sorted(bits[1:], reverse=True)
        for bit in order:
            part = halve(part, 1 + left.index(bit), bit)
            left.remove(bit)
        pieces.append(part)
    return jnp.concatenate(pieces, axis=0)


def sum_everywhere(vector):
    for bit in fsdp_bits():
        vector = vector + lax.ppermute(vector, "fsdp", partner(bit))
    for bit in (1, 2):
        vector = vector + lax.ppermute(vector, "tensor", [(i, i ^ bit) for i in range(4)])
    return vector


def nt(a, b):
    return lax.dot_general(a, b, (((1,), (1,)), ((), ())), preferred_element_type=F32)


def nn(a, b):
    return lax.dot_general(a, b, (((1,), (0,)), ((), ())), preferred_element_type=F32)


def tn(a, b):
    return lax.dot_general(a, b, (((0,), (0,)), ((), ())), preferred_element_type=F32)


def head_mask(shape, h):
    lane = lax.broadcasted_iota(jnp.int32, shape, len(shape) - 1)
    return (lane < HD) if h == 0 else (lane >= HD)


def forward_kernel(flags, q_ref, k_ref, v_ref, sq_ref, sk_ref, o_ref, lse_ref, m_s, l_s, acc_s):
    j = pl.program_id(1)
    nk = k_ref.shape[0] // BLOCK
    m_s[...] = jnp.full_like(m_s, MASKED)
    l_s[...] = jnp.zeros_like(l_s)
    acc_s[...] = jnp.zeros_like(acc_s)
    q = q_ref[...]
    seg_q = sq_ref[...]
    q_heads = [jnp.where(head_mask(q.shape, h), q, jnp.zeros_like(q)) for h in range(2)]
    for kb in range(nk):

        @pl.when(flags[j * nk + kb] != 0)
        def _():
            rows = pl.ds(kb * BLOCK, BLOCK)
            k = k_ref[rows, :]
            v = v_ref[rows, :]
            same = seg_q == sk_ref[:, rows]
            for h in range(2):
                s = nt(q_heads[h], k) * (HD**-0.5 * LOG2E)
                s = jnp.where(same, s, MASKED)
                m_old = m_s[h]
                m_new = jnp.maximum(m_old, jnp.max(s, axis=1, keepdims=True))
                alpha = jnp.exp2(m_old - m_new)
                p = jnp.exp2(s - m_new)
                l_s[h] = alpha * l_s[h] + jnp.sum(p, axis=1, keepdims=True)
                acc_s[h] = alpha * acc_s[h] + nn(p.astype(BF), v)
                m_s[h] = m_new

    out = [acc_s[h] / l_s[h] for h in range(2)]
    o_ref[...] = jnp.where(head_mask(out[0].shape, 0), out[0], out[1]).astype(o_ref.dtype)
    for h in range(2):
        lse = m_s[h] + jnp.log2(l_s[h])
        wide = jnp.broadcast_to(lse, (BLOCK, LANES)).T
        lse_ref[0, h : h + 1, :] = wide[0:1, :]


def attend_forward(q, k, v, seg_q, seg_k, flags):
    rows, width = q.shape
    keys = k.shape[0]
    pairs = width // LANES
    return pl.pallas_call(
        forward_kernel,
        out_shape=(
            jax.ShapeDtypeStruct((rows, width), BF),
            jax.ShapeDtypeStruct((pairs, 2, rows), F32),
        ),
        grid_spec=pltpu.PrefetchScalarGridSpec(
            num_scalar_prefetch=1,
            grid=(pairs, rows // BLOCK),
            in_specs=[
                pl.BlockSpec((BLOCK, LANES), lambda i, j, f: (j, i)),
                pl.BlockSpec((keys, LANES), lambda i, j, f: (0, i)),
                pl.BlockSpec((keys, LANES), lambda i, j, f: (0, i)),
                pl.BlockSpec((BLOCK, 1), lambda i, j, f: (j, 0)),
                pl.BlockSpec((1, keys), lambda i, j, f: (0, 0)),
            ],
            out_specs=[
                pl.BlockSpec((BLOCK, LANES), lambda i, j, f: (j, i)),
                pl.BlockSpec((1, 2, BLOCK), lambda i, j, f: (i, 0, j)),
            ],
            scratch_shapes=[
                pltpu.VMEM((2, BLOCK, 1), F32),
                pltpu.VMEM((2, BLOCK, 1), F32),
                pltpu.VMEM((2, BLOCK, LANES), F32),
            ],
        ),
        cost_estimate=pl.CostEstimate(
            flops=4 * rows * keys * width, bytes_accessed=4 * keys * width, transcendentals=rows * keys * width // HD
        ),
        name="attend_forward",
    )(flags, q, k, v, seg_q[:, None], seg_k[None, :])


def backward_kernel(
    flags, q_ref, k_ref, v_ref, do_ref, o_ref, lse_ref, sq_ref, sk_ref, dq_ref, dk_ref, dv_ref, dk_s, dv_s, dq_s
):
    j = pl.program_id(1)
    nk = k_ref.shape[0] // BLOCK

    @pl.when(j == 0)
    def _():
        dk_s[...] = jnp.zeros_like(dk_s)
        dv_s[...] = jnp.zeros_like(dv_s)

    dq_s[...] = jnp.zeros_like(dq_s)
    q = q_ref[...]
    do = do_ref[...]
    zero = jnp.zeros_like(q)
    masks = [head_mask(q.shape, h) for h in range(2)]
    q_heads = [jnp.where(m, q, zero) for m in masks]
    do_heads = [jnp.where(m, do, zero) for m in masks]
    prod = (do.astype(F32) * o_ref[...].astype(F32)).T
    delta = [jnp.sum(prod[h * HD : (h + 1) * HD], axis=0, keepdims=True) for h in range(2)]
    lse = [lse_ref[0, h : h + 1, :] for h in range(2)]
    seg_q = sq_ref[...]
    for kb in range(nk):

        @pl.when(flags[j * nk + kb] != 0)
        def _():
            rows = pl.ds(kb * BLOCK, BLOCK)
            k = k_ref[rows, :]
            v = v_ref[rows, :]
            same = sk_ref[rows, :] == seg_q
            dk = dk_s[rows, :]
            dv = dv_s[rows, :]
            dq = [None, None]
            for h in range(2):
                s = nt(k, q_heads[h]) * (HD**-0.5 * LOG2E)
                p = jnp.exp2(jnp.where(same, s - lse[h], MASKED))
                dp = nt(v, do_heads[h])
                ds = (p * (dp - delta[h])).astype(BF)
                dv = dv + nn(p.astype(BF), do_heads[h])
                dk = dk + nn(ds, q_heads[h])
                dq[h] = tn(ds, k)
            dk_s[rows, :] = dk
            dv_s[rows, :] = dv
            dq_s[...] += jnp.where(masks[0], dq[0], dq[1])

    dq_ref[...] = (dq_s[...] * HD**-0.5).astype(BF)

    @pl.when(j == pl.num_programs(1) - 1)
    def _():
        dk_ref[...] = (dk_s[...] * HD**-0.5).astype(BF)
        dv_ref[...] = dv_s[...].astype(BF)


def attend_backward(q, k, v, do, o, lse, seg_q, seg_k, flags):
    rows, width = q.shape
    keys = k.shape[0]
    pairs = width // LANES
    q_spec = pl.BlockSpec((BLOCK, LANES), lambda i, j, f: (j, i))
    k_spec = pl.BlockSpec((keys, LANES), lambda i, j, f: (0, i))
    return pl.pallas_call(
        backward_kernel,
        out_shape=(
            jax.ShapeDtypeStruct((rows, width), BF),
            jax.ShapeDtypeStruct((keys, width), BF),
            jax.ShapeDtypeStruct((keys, width), BF),
        ),
        grid_spec=pltpu.PrefetchScalarGridSpec(
            num_scalar_prefetch=1,
            grid=(pairs, rows // BLOCK),
            in_specs=[
                q_spec,
                k_spec,
                k_spec,
                q_spec,
                q_spec,
                pl.BlockSpec((1, 2, BLOCK), lambda i, j, f: (i, 0, j)),
                pl.BlockSpec((1, BLOCK), lambda i, j, f: (0, j)),
                pl.BlockSpec((keys, 1), lambda i, j, f: (0, 0)),
            ],
            out_specs=[q_spec, k_spec, k_spec],
            scratch_shapes=[
                pltpu.VMEM((keys, LANES), F32),
                pltpu.VMEM((keys, LANES), F32),
                pltpu.VMEM((BLOCK, LANES), F32),
            ],
        ),
        cost_estimate=pl.CostEstimate(
            flops=10 * rows * keys * width, bytes_accessed=8 * keys * width, transcendentals=rows * keys * width // HD
        ),
        name="attend_backward",
    )(flags, q, k, v, do, o, lse, seg_q[None, :], seg_k[:, None])


def overlap_flags(seg_q, seg_k):
    qb = seg_q.reshape(-1, BLOCK)
    kb = seg_k.reshape(-1, BLOCK)
    q_lo, q_hi = qb.min(axis=1), qb.max(axis=1)
    k_lo, k_hi = kb.min(axis=1), kb.max(axis=1)
    meet = (q_lo[:, None] <= k_hi[None, :]) & (k_lo[None, :] <= q_hi[:, None])
    return meet.astype(jnp.int32).reshape(-1)


def norm_parts(rows_in):
    mean = jnp.mean(rows_in, axis=-1, keepdims=True)
    centred = rows_in - mean
    spread = jnp.mean(centred * centred, axis=-1, keepdims=True)
    r = lax.rsqrt(spread + EPSILON)
    return centred * r, r


def norm_back(g_y, n, r, gain):
    e = g_y * gain
    g_s = r * (e - jnp.mean(e, axis=-1, keepdims=True) - n * jnp.mean(e * n, axis=-1, keepdims=True))
    return g_s, jnp.sum(g_y * n, axis=0), jnp.sum(g_y, axis=0)


def gelu_parts(u):
    c = 0.7978845608028654
    th = jnp.tanh(c * (u + 0.044715 * u * u * u))
    act = 0.5 * u * (1.0 + th)
    slope = 0.5 * (1.0 + th) + 0.5 * u * (1.0 - th * th) * c * (1.0 + 3 * 0.044715 * u * u)
    return act, slope


def on_device(
    tokens,
    segments,
    query_weight,
    query_bias,
    key_weight,
    value_weight,
    value_bias,
    mix_weight,
    mix_bias,
    norm_gain,
    norm_shift,
    up_weight,
    up_bias,
    down_weight,
    down_bias,
    final_gain,
    final_shift,
    out_grad,
):
    t = lax.axis_index("tensor")
    rows, width = tokens.shape
    units = up_weight.shape[1]
    parts = 4

    attn_shard = jnp.stack([query_weight, key_weight, value_weight, mix_weight.T])
    attn_line = jnp.concatenate(line_order(gather_line(attn_shard)), axis=2)
    x_slots = gather_line(tokens)
    up_line = jnp.stack(line_order(gather_line(up_weight)))
    down_line = jnp.stack(line_order(gather_line(down_weight.T)))
    attn_w = gather_fsdp(attn_line)
    up_w = gather_fsdp(up_line)
    down_w = gather_fsdp(down_line)

    x_all = jnp.concatenate(x_slots, axis=0)
    seg = jnp.where(segments == 0, 9, segments).reshape(parts, rows)
    slot_ids = slot_owner(t)
    seg_q = lax.dynamic_index_in_dim(seg, t, 0, keepdims=False)
    seg_k = jnp.concatenate([lax.dynamic_index_in_dim(seg, i, 0, keepdims=False) for i in slot_ids])
    flags = overlap_flags(seg_q, seg_k)
    wq, wk, wv, wm_t = (attn_w[i] for i in range(4))
    q = (nn(tokens, wq) + query_bias).astype(BF)
    k = nn(x_all, wk).astype(BF)
    v = (nn(x_all, wv) + value_bias).astype(BF)
    ctx, lse = attend_forward(q, k, v, seg_q, seg_k, flags)

    first_sum = tokens.astype(F32) + nt(ctx, wm_t) + mix_bias
    n1, r1 = norm_parts(first_sum)
    normed = n1 * norm_gain + norm_shift
    normed_low = normed.astype(BF)
    bias_blocks = up_bias.reshape(parts, units)
    pre = [nn(normed_low, up_w[i]) + bias_blocks[i] for i in range(parts)]
    act = [gelu_parts(u)[0].astype(BF) for u in pre]
    ffn = sum(nt(a, down_w[i]) for i, a in enumerate(act))
    second_sum = normed + ffn + down_bias
    n2, r2 = norm_parts(second_sum)
    layer_out = (n2 * final_gain + final_shift).astype(BF)

    g_out = out_grad.astype(F32) * jnp.where(seg_q < 9, 1.0, 0.0)[:, None]
    g_second, d_final_gain, d_final_shift = norm_back(g_out, n2, r2, final_gain)
    second_low = g_second.astype(BF)
    d_down = jnp.stack([tn(second_low, a).astype(BF) for a in act])
    g_pre = [
        (nn(second_low, down_w[i]) * gelu_parts(pre[i])[1]).astype(BF) for i in range(parts)
    ]
    d_up = jnp.stack([tn(normed_low, g).astype(BF) for g in g_pre])
    g_normed = g_second + sum(nt(g, up_w[i]) for i, g in enumerate(g_pre))
    g_first, d_norm_gain, d_norm_shift = norm_back(g_normed, n1, r1, norm_gain)
    first_low = g_first.astype(BF)
    g_ctx = nn(first_low, wm_t).astype(BF)
    d_mix = tn(first_low, ctx).astype(BF)

    d_down_f = reduce_fsdp(d_down)
    d_up_f = reduce_fsdp(d_up)

    early = sum_everywhere(
        jnp.concatenate(
            [
                jnp.sum(g_first, axis=0),
                d_norm_gain,
                d_norm_shift,
                jnp.sum(g_second, axis=0),
                d_final_gain,
                d_final_shift,
            ]
            + [jnp.sum(g.astype(F32), axis=0) for g in g_pre]
        )
    )

    dq, dk, dv = attend_backward(q, k, v, g_ctx, ctx, lse, seg_q, seg_k, flags)
    dx_part = nt(dk, wk) + nt(dv, wv)

    def dx_slot(slot):
        at = {"own": 0, "A": 1, "C": 2, "B": 3}[slot]
        block = dx_part[at * rows : (at + 1) * rows]
        if slot == "own":
            return block + g_first + nt(dq, wq)
        return block.astype(BF)

    tokens_grad = reduce_line(dx_slot)
    d_attn = jnp.stack(
        [tn(tokens, dq).astype(BF), tn(x_all, dk).astype(BF), tn(x_all, dv).astype(BF), d_mix]
    )
    d_attn_f = reduce_fsdp(d_attn)
    late = sum_everywhere(
        jnp.concatenate(
            [jnp.sum(dq.astype(F32), axis=0), jnp.sum(dv.astype(F32), axis=0)]
        )
    )

    def line_sum(blocks):
        ids = dict(zip(("own", "A", "C", "B"), slot_ids))
        return reduce_line(lambda s: lax.dynamic_index_in_dim(blocks, ids[s], 0, keepdims=False))

    down_grad = line_sum(d_down_f).T
    up_grad = line_sum(d_up_f)
    cols = width // parts
    attn_blocks = jnp.stack([d_attn_f[:, :, i * cols : (i + 1) * cols] for i in range(parts)])
    attn_grad = line_sum(attn_blocks)

    names = [
        early[i * width : (i + 1) * width] for i in range(6)
    ]
    return (
        layer_out,
        tokens_grad,
        attn_grad[0],
        late[:width],
        attn_grad[1],
        attn_grad[2],
        late[width:],
        attn_grad[3].T,
        names[0],
        names[1],
        names[2],
        up_grad,
        early[6 * width :],
        down_grad,
        names[3],
        names[4],
        names[5],
    )


def solution(mesh):
    both, rows_f, square, flipped = (
        P(("fsdp", "tensor"), None),
        P("fsdp", None),
        P("fsdp", "tensor"),
        P("tensor", "fsdp"),
    )
    return jax.shard_map(
        on_device,
        mesh=mesh,
        in_specs=(
            both, rows_f, square, P(), square, square, P(), flipped, P(), P(), P(),
            square, P(), flipped, P(), P(), P(), both,
        ),
        out_specs=(
            both, both, square, P(), square, square, P(), flipped, P(), P(), P(),
            square, P(), flipped, P(), P(), P(),
        ),
        check_vma=False,
    )
```

time: 1120 us -> 578 us (0.52)
  waiting for transfers between devices: 668 us -> 129 us
  starting transfers between devices: 8.8 us -> 247 us
  matrix products: 213 us -> 68.5 us
  blocking collectives: 93.3 us -> 0 us
  Pallas kernels: 0 us -> 71.7 us
  other arithmetic: 86.2 us -> 27.8 us
  between operations: 16.7 us -> 3.34 us
    reduce_scatter x6 -> x0, waiting for transfers between devices: 435 us -> none  [the longest x4 344 us: reduce_rows(): lax.psum_scatter(reduce(jnp.add, products), 'tensor', scatter_dimension=0...]
    ppermute x0 -> x83, starting transfers between devices: none -> 247 us  [the longest x6 50.5 us: sum_everywhere(): vector = vector + lax.ppermute(vector, 'fsdp', partner(bit))]
    all_gather x6 -> x0, waiting for transfers between devices: 228 us -> none  [the longest x4 214 us: gather_rows(): return lax.all_gather(local_rows, 'tensor', axis=0, tiled=True)]
    dot_general x46 -> x36, matrix products: 213 us -> 68.5 us  [the longest x12 27 us: nn(): lax.dot_general(a, b, (((1,), (0,)), ((), ())), preferred_element_type=F32)]
    ppermute x0 -> x83, waiting for transfers between devices: none -> 129 us  [the longest x15 38.1 us: halve(): got = lax.ppermute(send, 'fsdp', partner(bit))]
    pallas_call x0 -> x2, Pallas kernels: none -> 71.7 us  [the longest x1 39.9 us: attend_forward(): pl.pallas_call(forward_kernel, out_shape=(jax.ShapeDtypeStruct((rows, wid...]
    psum x1 -> x0, blocking collectives: 54.4 us -> none  [on_device(): lax.psum((query_bias_part, value_bias_part, jnp.sum(grad_first, axis=0),...]
    reduce_sum x18 -> x7, other arithmetic: 46 us -> 4.86 us  [the longest x1 1.61 us: on_device(): jnp.sum(g_second, axis=0)]
  transfers between devices with their start and end apart: 14 -> 83, of which waited for: 12 -> 24; matrix products, arithmetic and copies ran while one was open for 5% -> 10% of each run, Pallas kernels for 0% -> 7%
where the time goes in v1:
time: 578 us; the launch traced here: 577 us
  starting transfers between devices  247 us (43%)
  waiting for transfers between devices  129 us (22%)
  Pallas kernels  71.7 us (12%)
  matrix products  68.5 us (12%)
  local copies, waits for them, and re-layouts  29.5 us (5%)
  other arithmetic  27.8 us (5%)
    ppermute x6, starting transfers between devices, sum_everywhere(): vector = vector + lax.ppermute(vector, 'fsdp', partner(bit))  50.5 us
    ppermute x15, starting transfers between devices, halve(): got = lax.ppermute(send, 'fsdp', partner(bit))  42.5 us
    pallas_call x1, Pallas kernels, attend_forward(): pl.pallas_call(forward_kernel, out_shape=(jax.ShapeDtypeStruct((rows, wid...  39.9 us
    ppermute x15, waiting for transfers between devices, halve(): got = lax.ppermute(send, 'fsdp', partner(bit))  38.1 us
    ppermute x18, waiting for transfers between devices, grow(): other = lax.ppermute(block, 'fsdp', partner(bit))  35.6 us
    pallas_call x1, Pallas kernels, attend_backward(): pl.pallas_call(backward_kernel, out_shape=(jax.ShapeDtypeStruct((rows, wi...  31.8 us
    ppermute x4, starting transfers between devices, reduce_line(): rx = lax.ppermute(c, 'tensor', ends).astype(F32)  27.3 us
    ppermute x4, starting transfers between devices, gather_line(): below = lax.ppermute(own, 'tensor', [(0, 1), (1, 2), (2, 3)])  27.1 us
  transfers between devices with their start and end apart: 83, of which 24 were waited for; matrix products, arithmetic and copies ran while one was open for 10% of the time, Pallas kernels for 7%

profile of v1, /device:TPU:0, one launch (start us, length us, event | category | flops | bytes accessed | tf_op | source)
XLA Modules:
  0.0 576.9 jit_solution(1939023248116980280)
XLA Ops:
  2.0 5.6 collective-permute-start.26
  8.8 4.6 collective-permute-start.18
  24.6 8.4 %collective-permute-start.2 = (bf16[4,96,192]{2,1,0:T(8,128)(2,1)S(1)}, bf16[4,96,192]{2,1,0:T(8,128)(2,1)S(1)}, u32[]{:S(2)}, u32[]{:S(2)}) collective-permute-start(bf16[4,96,192]{2,1,0:T(8,128)(2,1)S(1)} %pad_maximum_fusion.23), channel_id=1, source_target_pairs={{0,1},{1,2},{2,3},{4,5},{5,6},{6,7},{8,9},{9,10},{10,11},{12,13},{... | collective-permute-start | bytes 442376 | tf_op jit(solution)/shard_map/ppermute | solution.py:22
  36.4 8.5 %collective-permute-start.9 = (bf16[512,768]{1,0:T(8,128)(2,1)}, bf16[512,768]{1,0:T(8,128)(2,1)S(1)}, u32[]{:S(2)}, u32[]{:S(2)}) collective-permute-start(bf16[512,768]{1,0:T(8,128)(2,1)} %param.18), channel_id=1, source_target_pairs={{0,1},{1,2},{2,3},{4,5},{5,6},{6,7},{8,9},{9,10},{10,11},{12,13},{... | collective-permute-start | bytes 2359304 | tf_op jit(solution)/shard_map/ppermute | solution.py:22
  46.2 11.6 %collective-permute-done.17 = bf16[96,768]{1,0:T(8,128)(2,1)S(1)} collective-permute-done((bf16[96,768]{1,0:T(8,128)(2,1)S(1)}, bf16[96,768]{1,0:T(8,128)(2,1)S(1)}, u32[]{:S(2)}, u32[]{:S(2)}) %collective-permute-start.17) | collective-permute-done | bytes 147488 | tf_op jit(solution)/shard_map/ppermute | solution.py:26
  66.8 2.4 collective-permute-start.35
  73.9 2.4 collective-permute-done.35
  76.3 2.3 collective-permute-start.5
  88.6 3.9 collective-permute-done.29
  95.1 3.8 collective-permute-done.21
  101.2 10.3 %collective-permute-done.36 = bf16[2,2,96,768]{3,2,1,0:T(8,128)(2,1)S(1)} collective-permute-done((bf16[2,2,96,768]{3,2,1,0:T(8,128)(2,1)S(1)}, bf16[2,2,96,768]{3,2,1,0:T(8,128)(2,1)S(1)}, u32[]{:S(2)}, u32[]{:S(2)}) %collective-permute-start.36) | collective-permute-done | bytes 589856 | tf_op jit(solution)/shard_map/ppermute | solution.py:85
  117.7 6.5 %collective-permute-done.14 = bf16[2,2,96,768]{3,2,1,0:T(8,128)(2,1)S(1)} collective-permute-done((bf16[2,2,96,768]{3,2,1,0:T(8,128)(2,1)S(1)}, bf16[2,2,96,768]{3,2,1,0:T(8,128)(2,1)S(1)}, u32[]{:S(2)}, u32[]{:S(2)}) %collective-permute-start.14) | collective-permute-done | bytes 589856 | tf_op jit(solution)/shard_map/ppermute | solution.py:85
  126.5 4.2 collective-permute-done.33
  135.7 17.3 %collective-permute-done.12 = bf16[512,768]{1,0:T(8,128)(2,1)S(1)} collective-permute-done((bf16[512,768]{1,0:T(8,128)(2,1)S(1)}, bf16[512,768]{1,0:T(8,128)(2,1)S(1)}, u32[]{:S(2)}, u32[]{:S(2)}) %collective-permute-start.12) | collective-permute-done | bytes 786464 | tf_op jit(solution)/shard_map/ppermute | solution.py:28
  162.7 2.9 fusion.41.q_ref
  165.6 5.4 convolution_convert_fusion.k_ref
  171.1 5.5 add_convert_fusion.v_ref
  176.5 39.9 %attend_forward.1 = (bf16[512,768]{1,0:T(8,128)(2,1)}, f32[6,2,512]{2,1,0:T(2,128)}) custom-call(s32[16]{0:T(128)} %reshape.235.flags, bf16[512,768]{1,0:T(8,128)(2,1)} %fusion.41.q_ref, bf16[2048,768]{1,0:T(8,128)(2,1)} %convolution_convert_fusion.k_ref, bf16[2048,768]{1,0:T(8,128)(2,1)} %add_convert_fusion.v_ref, s32[512,1]{1,0:T(8,128)} %copy.60.sq_ref, ...), custom_call_target="tpu_custom_call" | custom-call | flops 3221225472 | bytes 6291456 | tf_op jit(solution)/shard_map/attend_forward/pallas_call | solution.py:203
  216.5 2.6 fusion.132
  254.0 31.8 %attend_backward.1 = (bf16[512,768]{1,0:T(8,128)(2,1)}, bf16[2048,768]{1,0:T(8,128)(2,1)}, bf16[2048,768]{1,0:T(8,128)(2,1)}) custom-call(s32[16]{0:T(128)} %reshape.235.flags, bf16[512,768]{1,0:T(8,128)(2,1)} %fusion.41.q_ref, bf16[2048,768]{1,0:T(8,128)(2,1)} %convolution_convert_fusion.k_ref, bf16[2048,768]{1,0:T(8,128)(2,1)} %add_convert_fusion.v_ref, ...), custom_call_target="tpu_custom_call" | custom-call | flops 8053063680 | bytes 12582912 | tf_op jit(solution)/shard_map/attend_backward/pallas_call | solution.py:295
  285.8 5.2 fusion.138
  291.1 4.0 convolution_convert_fusion.11
  295.0 3.9 convolution_convert_fusion.10
  300.0 3.1 convolution_convert_fusion.12
  313.4 2.6 fusion.134
  316.1 13.5 %collective-permute-start.38 = (bf16[512,768]{1,0:T(8,128)(2,1)S(1)}, bf16[512,768]{1,0:T(8,128)(2,1)}, u32[]{:S(2)}, u32[]{:S(2)}) collective-permute-start(bf16[512,768]{1,0:T(8,128)(2,1)S(1)} %slice.232), channel_id=1, source_target_pairs={{0,1},{3,2},{4,5},{7,6},{8,9},{11,10},{12,13},{15,14},{16,17},{19,... | collective-permute-start | bytes 2359304 | tf_op jit(solution)/shard_map/ppermute | solution.py:61
  332.3 32.7 %collective-permute-start.43 = (bf16[4,2,2,96,768]{4,3,0,2,1:T(8,128)(2,1)}, bf16[4,2,2,96,768]{4,3,0,2,1:T(8,128)(2,1)S(1)}, u32[]{:S(2)}, u32[]{:S(2)}) collective-permute-start(bf16[4,2,2,96,768]{4,3,0,2,1:T(8,128)(2,1)} %bitcast.365), channel_id=1, source_target_pairs={{0,4},{4,0},{8,12},{12,8},{16,20},{20,16},{24,28},{28,24},{1,5},{5... | collective-permute-start | bytes 7077896 | tf_op jit(solution)/shard_map/ppermute | solution.py:116
  370.4 17.7 %collective-permute-start.39 = (bf16[512,768]{1,0:T(8,128)(2,1)}, bf16[512,768]{1,0:T(8,128)(2,1)S(1)}, u32[]{:S(2)}, u32[]{:S(2)}) collective-permute-start(bf16[512,768]{1,0:T(8,128)(2,1)} %add_convert_fusion.1), channel_id=1, source_target_pairs={{0,1},{3,2},{4,5},{7,6},{8,9},{11,10},{12,13},{15,14},{16,17},{19,... | collective-permute-start | bytes 2359304 | tf_op jit(solution)/shard_map/ppermute | solution.py:63
  388.2 8.2 %collective-permute-start.54 = (f32[1536]{0:T(1024)S(1)}, f32[1536]{0:T(1024)S(1)}, u32[]{:S(2)}, u32[]{:S(2)}) collective-permute-start(f32[1536]{0:T(1024)S(1)} %fusion.108), channel_id=1, source_target_pairs={{0,8},{4,12},{8,0},{12,4},{16,24},{20,28},{24,16},{28,20},{1,9},{5... | collective-permute-start | bytes 18440 | tf_op jit(solution)/shard_map/ppermute | solution.py:140
  396.4 5.8 collective-permute-start.58
  402.2 28.7 %collective-permute-start.55 = (f32[1536]{0:T(1024)S(1)}, f32[1536]{0:T(1024)S(1)}, u32[]{:S(2)}, u32[]{:S(2)}) collective-permute-start(f32[1536]{0:T(1024)S(1)} %add.480), channel_id=1, source_target_pairs={{0,16},{4,20},{8,24},{12,28},{16,0},{20,4},{24,8},{28,12},{1,17},{... | collective-permute-start | bytes 18440 | tf_op jit(solution)/shard_map/ppermute | solution.py:140
  438.0 7.7 %collective-permute-start.60 = (f32[7680]{0:T(1024)S(1)}, f32[7680]{0:T(1024)S(1)}, u32[]{:S(2)}, u32[]{:S(2)}) collective-permute-start(f32[7680]{0:T(1024)S(1)} %add.485), channel_id=1, source_target_pairs={{0,16},{4,20},{8,24},{12,28},{16,0},{20,4},{24,8},{28,12},{1,17},{... | collective-permute-start | bytes 92168 | tf_op jit(solution)/shard_map/ppermute | solution.py:140
  447.6 4.8 collective-permute-start.41
  454.2 15.4 %collective-permute-done.61 = f32[7680]{0:T(1024)S(1)} collective-permute-done((f32[7680]{0:T(1024)S(1)}, f32[7680]{0:T(1024)S(1)}, u32[]{:S(2)}, u32[]{:S(2)}) %collective-permute-start.61) | collective-permute-done | bytes 30752 | tf_op jit(solution)/shard_map/ppermute | solution.py:142
  470.9 3.4 collective-permute-done.62
  484.8 9.6 %collective-permute-done.44 = bf16[2,2,96,768]{3,2,0,1:T(8,128)(2,1)S(1)} collective-permute-done((bf16[2,2,96,768]{3,2,0,1:T(8,128)(2,1)S(1)}, bf16[2,2,96,768]{3,2,0,1:T(8,128)(2,1)S(1)}, u32[]{:S(2)}, u32[]{:S(2)}) %collective-permute-start.44) | collective-permute-done | bytes 589856 | tf_op jit(solution)/shard_map/ppermute | solution.py:116
  496.9 10.2 %collective-permute-done.64 = bf16[2,2,96,768]{3,2,0,1:T(8,128)(2,1)S(1)} collective-permute-done((bf16[2,2,96,768]{3,2,0,1:T(8,128)(2,1)S(1)}, bf16[2,2,96,768]{3,2,0,1:T(8,128)(2,1)S(1)}, u32[]{:S(2)}, u32[]{:S(2)}) %collective-permute-start.64) | collective-permute-done | bytes 589856 | tf_op jit(solution)/shard_map/ppermute | solution.py:116
  508.2 11.6 %collective-permute-done.74 = bf16[2,2,96,768]{3,2,0,1:T(8,128)(2,1)S(1)} collective-permute-done((bf16[2,2,96,768]{3,2,0,1:T(8,128)(2,1)S(1)}, bf16[2,2,96,768]{3,2,0,1:T(8,128)(2,1)S(1)}, u32[]{:S(2)}, u32[]{:S(2)}) %collective-permute-start.74) | collective-permute-done | bytes 589856 | tf_op jit(solution)/shard_map/ppermute | solution.py:116
  520.8 5.4 collective-permute-done.45
  528.8 4.4 collective-permute-start.48
  533.5 3.7 collective-permute-start.68
  538.7 4.4 collective-permute-start.78
  543.9 2.5 collective-permute-start.49
  547.2 4.5 collective-permute-start.69
  552.6 2.5 collective-permute-start.79
  556.6 4.6 collective-permute-start.51
  562.6 4.6 collective-permute-start.71
  568.7 4.6 collective-permute-start.81
  (491 shorter events, 164.8 us)
Async XLA Ops:
  0.7 21.9 %collective-permute-start.24 = (bf16[96,768]{1,0:T(8,128)(2,1)}, bf16[96,768]{1,0:T(8,128)(2,1)S(1)}, u32[]{:S(2)}, u32[]{:S(2)}) collective-permute-start(bf16[96,768]{1,0:T(8,128)(2,1)} %bitcast.374), channel_id=1, source_target_pairs={{1,0},{2,1},{3,2},{5,4},{6,5},{7,6},{9,8},{10,9},{11,10},{13,12},{... | collective-permute-start | bytes 442376 | tf_op jit(solution)/shard_map/ppermute | solution.py:23
  2.0 21.9 %collective-permute-start.26 = (bf16[96,768]{1,0:T(8,128)(2,1)}, bf16[96,768]{1,0:T(8,128)(2,1)S(1)}, u32[]{:S(2)}, u32[]{:S(2)}) collective-permute-start(bf16[96,768]{1,0:T(8,128)(2,1)} %bitcast.375), channel_id=1, source_target_pairs={{0,1},{1,2},{2,3},{4,5},{5,6},{6,7},{8,9},{9,10},{10,11},{12,13},{... | collective-permute-start | bytes 442376 | tf_op jit(solution)/shard_map/ppermute | solution.py:22
  7.5 17.0 %collective-permute-start.16 = (bf16[96,768]{1,0:T(8,128)(2,1)}, bf16[96,768]{1,0:T(8,128)(2,1)S(1)}, u32[]{:S(2)}, u32[]{:S(2)}) collective-permute-start(bf16[96,768]{1,0:T(8,128)(2,1)} %param.29), channel_id=1, source_target_pairs={{1,0},{2,1},{3,2},{5,4},{6,5},{7,6},{9,8},{10,9},{11,10},{13,12},{... | collective-permute-start | bytes 442376 | tf_op jit(solution)/shard_map/ppermute | solution.py:23
  8.8 24.2 %collective-permute-start.18 = (bf16[96,768]{1,0:T(8,128)(2,1)}, bf16[96,768]{1,0:T(8,128)(2,1)S(1)}, u32[]{:S(2)}, u32[]{:S(2)}) collective-permute-start(bf16[96,768]{1,0:T(8,128)(2,1)} %param.29), channel_id=1, source_target_pairs={{0,1},{1,2},{2,3},{4,5},{5,6},{6,7},{8,9},{9,10},{10,11},{12,13},{... | collective-permute-start | bytes 442376 | tf_op jit(solution)/shard_map/ppermute | solution.py:22
  15.2 21.2 %collective-permute-start = (bf16[4,96,192]{2,1,0:T(8,128)(2,1)S(1)}, bf16[4,96,192]{2,1,0:T(8,128)(2,1)S(1)}, u32[]{:S(2)}, u32[]{:S(2)}) collective-permute-start(bf16[4,96,192]{2,1,0:T(8,128)(2,1)S(1)} %pad_maximum_fusion.23), channel_id=1, source_target_pairs={{1,0},{2,1},{3,2},{5,4},{6,5},{7,6},{9,8},{10,9},{11,10},{13,12},{... | collective-permute-start | bytes 442376 | tf_op jit(solution)/shard_map/ppermute | solution.py:23
  24.6 20.3 %collective-permute-start.2 = (bf16[4,96,192]{2,1,0:T(8,128)(2,1)S(1)}, bf16[4,96,192]{2,1,0:T(8,128)(2,1)S(1)}, u32[]{:S(2)}, u32[]{:S(2)}) collective-permute-start(bf16[4,96,192]{2,1,0:T(8,128)(2,1)S(1)} %pad_maximum_fusion.23), channel_id=1, source_target_pairs={{0,1},{1,2},{2,3},{4,5},{5,6},{6,7},{8,9},{9,10},{10,11},{12,13},{... | collective-permute-start | bytes 442376 | tf_op jit(solution)/shard_map/ppermute | solution.py:22
  33.1 80.8 %collective-permute-start.8 = (bf16[512,768]{1,0:T(8,128)(2,1)}, bf16[512,768]{1,0:T(8,128)(2,1)S(1)}, u32[]{:S(2)}, u32[]{:S(2)}) collective-permute-start(bf16[512,768]{1,0:T(8,128)(2,1)} %param.18), channel_id=1, source_target_pairs={{1,0},{2,1},{3,2},{5,4},{6,5},{7,6},{9,8},{10,9},{11,10},{13,12},{... | collective-permute-start | bytes 2359304 | tf_op jit(solution)/shard_map/ppermute | solution.py:23
  34.4 23.4 %collective-permute-start.17 = (bf16[96,768]{1,0:T(8,128)(2,1)S(1)}, bf16[96,768]{1,0:T(8,128)(2,1)S(1)}, u32[]{:S(2)}, u32[]{:S(2)}) collective-permute-start(bf16[96,768]{1,0:T(8,128)(2,1)S(1)} %collective-permute-done.16), channel_id=1, source_target_pairs={{2,1},{1,0},{6,5},{5,4},{10,9},{9,8},{14,13},{13,12},{18,17},{17,1... | collective-permute-start | bytes 442376 | tf_op jit(solution)/shard_map/ppermute | solution.py:26
  35.7 22.7 %collective-permute-start.19 = (bf16[96,768]{1,0:T(8,128)(2,1)S(1)}, bf16[96,768]{1,0:T(8,128)(2,1)S(1)}, u32[]{:S(2)}, u32[]{:S(2)}) collective-permute-start(bf16[96,768]{1,0:T(8,128)(2,1)S(1)} %collective-permute-done.18), channel_id=1, source_target_pairs={{1,2},{2,3},{5,6},{6,7},{9,10},{10,11},{13,14},{14,15},{17,18},{18... | collective-permute-start | bytes 442376 | tf_op jit(solution)/shard_map/ppermute | solution.py:25
  36.4 79.0 %collective-permute-start.9 = (bf16[512,768]{1,0:T(8,128)(2,1)}, bf16[512,768]{1,0:T(8,128)(2,1)S(1)}, u32[]{:S(2)}, u32[]{:S(2)}) collective-permute-start(bf16[512,768]{1,0:T(8,128)(2,1)} %param.18), channel_id=1, source_target_pairs={{0,1},{1,2},{2,3},{4,5},{5,6},{6,7},{8,9},{9,10},{10,11},{12,13},{... | collective-permute-start | bytes 2359304 | tf_op jit(solution)/shard_map/ppermute | solution.py:22
  44.9 16.6 %collective-permute-start.1 = (bf16[4,96,192]{2,1,0:T(8,128)(2,1)S(1)}, bf16[4,96,192]{2,1,0:T(8,128)(2,1)S(1)}, u32[]{:S(2)}, u32[]{:S(2)}) collective-permute-start(bf16[4,96,192]{2,1,0:T(8,128)(2,1)S(1)} %collective-permute-done), channel_id=1, source_target_pairs={{2,1},{1,0},{6,5},{5,4},{10,9},{9,8},{14,13},{13,12},{18,17},{17,1... | collective-permute-start | bytes 442376 | tf_op jit(solution)/shard_map/ppermute | solution.py:26
  86.8 24.7 %collective-permute-start.36 = (bf16[2,2,96,768]{3,2,1,0:T(8,128)(2,1)S(1)}, bf16[2,2,96,768]{3,2,1,0:T(8,128)(2,1)S(1)}, u32[]{:S(2)}, u32[]{:S(2)}) collective-permute-start(bf16[2,2,96,768]{3,2,1,0:T(8,128)(2,1)S(1)} %pad_maximum_fusion.17), channel_id=1, source_target_pairs={{0,8},{4,12},{8,0},{12,4},{16,24},{20,28},{24,16},{28,20},{1,9},{5... | collective-permute-start | bytes 1769480 | tf_op jit(solution)/shard_map/ppermute | solution.py:85
  92.5 24.2 %collective-permute-start.6 = (bf16[2,2,96,768]{3,2,0,1:T(8,128)(2,1)S(1)}, bf16[2,2,96,768]{3,2,0,1:T(8,128)(2,1)S(1)}, u32[]{:S(2)}, u32[]{:S(2)}) collective-permute-start(bf16[2,2,96,768]{3,2,0,1:T(8,128)(2,1)S(1)} %pad_maximum_fusion.12), channel_id=1, source_target_pairs={{0,16},{4,20},{8,24},{12,28},{16,0},{20,4},{24,8},{28,12},{1,17},{... | collective-permute-start | bytes 1769480 | tf_op jit(solution)/shard_map/ppermute | solution.py:85
  98.8 25.3 %collective-permute-start.14 = (bf16[2,2,96,768]{3,2,1,0:T(8,128)(2,1)S(1)}, bf16[2,2,96,768]{3,2,1,0:T(8,128)(2,1)S(1)}, u32[]{:S(2)}, u32[]{:S(2)}) collective-permute-start(bf16[2,2,96,768]{3,2,1,0:T(8,128)(2,1)S(1)} %pad_maximum_fusion.13), channel_id=1, source_target_pairs={{0,8},{4,12},{8,0},{12,4},{16,24},{20,28},{24,16},{28,20},{1,9},{5... | collective-permute-start | bytes 1769480 | tf_op jit(solution)/shard_map/ppermute | solution.py:85
  111.5 19.2 %collective-permute-start.33 = (bf16[2,2,96,768]{3,2,1,0:T(8,128)(2,1)S(1)}, bf16[2,2,96,768]{3,2,1,0:T(8,128)(2,1)S(1)}, u32[]{:S(2)}, u32[]{:S(2)}) collective-permute-start(bf16[2,2,96,768]{3,2,1,0:T(8,128)(2,1)S(1)} %pad_maximum_fusion.16), channel_id=1, source_target_pairs={{0,8},{4,12},{8,0},{12,4},{16,24},{20,28},{24,16},{28,20},{1,9},{5... | collective-permute-start | bytes 1769480 | tf_op jit(solution)/shard_map/ppermute | solution.py:85
  113.8 19.5 %collective-permute-start.30 = (bf16[2,2,96,768]{3,2,1,0:T(8,128)(2,1)S(1)}, bf16[2,2,96,768]{3,2,1,0:T(8,128)(2,1)S(1)}, u32[]{:S(2)}, u32[]{:S(2)}) collective-permute-start(bf16[2,2,96,768]{3,2,1,0:T(8,128)(2,1)S(1)} %pad_maximum_fusion.15), channel_id=1, source_target_pairs={{0,16},{4,20},{8,24},{12,28},{16,0},{20,4},{24,8},{28,12},{1,17},{... | collective-permute-start | bytes 1769480 | tf_op jit(solution)/shard_map/ppermute | solution.py:85
  115.4 15.5 %collective-permute-start.10 = (bf16[512,768]{1,0:T(8,128)(2,1)S(1)}, bf16[512,768]{1,0:T(8,128)(2,1)S(1)}, u32[]{:S(2)}, u32[]{:S(2)}) collective-permute-start(bf16[512,768]{1,0:T(8,128)(2,1)S(1)} %collective-permute-done.8), channel_id=1, source_target_pairs={{2,1},{1,0},{6,5},{5,4},{10,9},{9,8},{14,13},{13,12},{18,17},{17,1... | collective-permute-start | bytes 2359304 | tf_op jit(solution)/shard_map/ppermute | solution.py:26
  116.7 14.8 %collective-permute-start.11 = (bf16[512,768]{1,0:T(8,128)(2,1)S(1)}, bf16[512,768]{1,0:T(8,128)(2,1)S(1)}, u32[]{:S(2)}, u32[]{:S(2)}) collective-permute-start(bf16[512,768]{1,0:T(8,128)(2,1)S(1)} %collective-permute-done.9), channel_id=1, source_target_pairs={{1,2},{2,3},{5,6},{6,7},{9,10},{10,11},{13,14},{14,15},{17,18},{18... | collective-permute-start | bytes 2359304 | tf_op jit(solution)/shard_map/ppermute | solution.py:25
  130.7 22.4 %collective-permute-start.37 = (bf16[2,2,2,96,768]{4,3,2,1,0:T(8,128)(2,1)S(1)}, bf16[2,2,2,96,768]{4,3,2,1,0:T(8,128)(2,1)S(1)}, u32[]{:S(2)}, u32[]{:S(2)}) collective-permute-start(bf16[2,2,2,96,768]{4,3,2,1,0:T(8,128)(2,1)S(1)} %pad_maximum_fusion.9), channel_id=1, source_target_pairs={{0,4},{4,0},{8,12},{12,8},{16,20},{20,16},{24,28},{28,24},{1,5},{5... | collective-permute-start | bytes 3538952 | tf_op jit(solution)/shard_map/ppermute | solution.py:85
  130.9 28.3 %collective-permute-start.7 = (bf16[2,2,2,96,768]{4,3,1,0,2:T(8,128)(2,1)S(1)}, bf16[2,2,2,96,768]{4,3,1,0,2:T(8,128)(2,1)S(1)}, u32[]{:S(2)}, u32[]{:S(2)}) collective-permute-start(bf16[2,2,2,96,768]{4,3,1,0,2:T(8,128)(2,1)S(1)} %pad_maximum_fusion.4), channel_id=1, source_target_pairs={{0,4},{4,0},{8,12},{12,8},{16,20},{20,16},{24,28},{28,24},{1,5},{5... | collective-permute-start | bytes 3538952 | tf_op jit(solution)/shard_map/ppermute | solution.py:85
  131.6 21.4 %collective-permute-start.12 = (bf16[512,768]{1,0:T(8,128)(2,1)S(1)}, bf16[512,768]{1,0:T(8,128)(2,1)S(1)}, u32[]{:S(2)}, u32[]{:S(2)}) collective-permute-start(bf16[512,768]{1,0:T(8,128)(2,1)S(1)} %broadcast_select_fusion.1), channel_id=1, source_target_pairs={{1,0},{2,3},{5,4},{6,7},{9,8},{10,11},{13,12},{14,15},{17,16},{18,... | collective-permute-start | bytes 2359304 | tf_op jit(solution)/shard_map/ppermute | solution.py:28
  133.3 20.9 %collective-permute-start.15 = (bf16[2,2,2,96,768]{4,3,2,1,0:T(8,128)(2,1)S(1)}, bf16[2,2,2,96,768]{4,3,2,1,0:T(8,128)(2,1)S(1)}, u32[]{:S(2)}, u32[]{:S(2)}) collective-permute-start(bf16[2,2,2,96,768]{4,3,2,1,0:T(8,128)(2,1)S(1)} %pad_maximum_fusion.5), channel_id=1, source_target_pairs={{0,4},{4,0},{8,12},{12,8},{16,20},{20,16},{24,28},{28,24},{1,5},{5... | collective-permute-start | bytes 3538952 | tf_op jit(solution)/shard_map/ppermute | solution.py:85
  134.3 20.6 %collective-permute-start.34 = (bf16[2,2,2,96,768]{4,3,2,1,0:T(8,128)(2,1)S(1)}, bf16[2,2,2,96,768]{4,3,2,1,0:T(8,128)(2,1)S(1)}, u32[]{:S(2)}, u32[]{:S(2)}) collective-permute-start(bf16[2,2,2,96,768]{4,3,2,1,0:T(8,128)(2,1)S(1)} %pad_maximum_fusion.8), channel_id=1, source_target_pairs={{0,4},{4,0},{8,12},{12,8},{16,20},{20,16},{24,28},{28,24},{1,5},{5... | collective-permute-start | bytes 3538952 | tf_op jit(solution)/shard_map/ppermute | solution.py:85
  153.1 66.3 %collective-permute-start.23 = (bf16[2,2,2,96,768]{4,3,2,1,0:T(8,128)(2,1)}, bf16[2,2,2,96,768]{4,3,2,1,0:T(8,128)(2,1)}, u32[]{:S(2)}, u32[]{:S(2)}) collective-permute-start(bf16[2,2,2,96,768]{4,3,2,1,0:T(8,128)(2,1)} %pad_maximum_fusion.6), channel_id=1, source_target_pairs={{0,4},{4,0},{8,12},{12,8},{16,20},{20,16},{24,28},{28,24},{1,5},{5... | collective-permute-start | bytes 3538952 | tf_op jit(solution)/shard_map/ppermute | solution.py:85
  316.1 51.3 %collective-permute-start.38 = (bf16[512,768]{1,0:T(8,128)(2,1)S(1)}, bf16[512,768]{1,0:T(8,128)(2,1)}, u32[]{:S(2)}, u32[]{:S(2)}) collective-permute-start(bf16[512,768]{1,0:T(8,128)(2,1)S(1)} %slice.232), channel_id=1, source_target_pairs={{0,1},{3,2},{4,5},{7,6},{8,9},{11,10},{12,13},{15,14},{16,17},{19,... | collective-permute-start | bytes 2359304 | tf_op jit(solution)/shard_map/ppermute | solution.py:61
  332.3 145.0 %collective-permute-start.43 = (bf16[4,2,2,96,768]{4,3,0,2,1:T(8,128)(2,1)}, bf16[4,2,2,96,768]{4,3,0,2,1:T(8,128)(2,1)S(1)}, u32[]{:S(2)}, u32[]{:S(2)}) collective-permute-start(bf16[4,2,2,96,768]{4,3,0,2,1:T(8,128)(2,1)} %bitcast.365), channel_id=1, source_target_pairs={{0,4},{4,0},{8,12},{12,8},{16,20},{20,16},{24,28},{28,24},{1,5},{5... | collective-permute-start | bytes 7077896 | tf_op jit(solution)/shard_map/ppermute | solution.py:116
  365.0 23.2 %collective-permute-start.53 = (f32[1536]{0:T(1024)S(1)}, f32[1536]{0:T(1024)S(1)}, u32[]{:S(2)}, u32[]{:S(2)}) collective-permute-start(f32[1536]{0:T(1024)S(1)} %pad_maximum_fusion.24), channel_id=1, source_target_pairs={{0,4},{4,0},{8,12},{12,8},{16,20},{20,16},{24,28},{28,24},{1,5},{5... | collective-permute-start | bytes 18440 | tf_op jit(solution)/shard_map/ppermute | solution.py:140
  369.7 68.3 %collective-permute-start.40 = (bf16[512,768]{1,0:T(8,128)(2,1)}, bf16[512,768]{1,0:T(8,128)(2,1)S(1)}, u32[]{:S(2)}, u32[]{:S(2)}) collective-permute-start(bf16[512,768]{1,0:T(8,128)(2,1)} %add_convert_fusion.1), channel_id=1, source_target_pairs={{1,2},{2,1},{5,6},{6,5},{9,10},{10,9},{13,14},{14,13},{17,18},{18,... | collective-permute-start | bytes 2359304 | tf_op jit(solution)/shard_map/ppermute | solution.py:64
  370.4 75.3 %collective-permute-start.39 = (bf16[512,768]{1,0:T(8,128)(2,1)}, bf16[512,768]{1,0:T(8,128)(2,1)S(1)}, u32[]{:S(2)}, u32[]{:S(2)}) collective-permute-start(bf16[512,768]{1,0:T(8,128)(2,1)} %add_convert_fusion.1), channel_id=1, source_target_pairs={{0,1},{3,2},{4,5},{7,6},{8,9},{11,10},{12,13},{15,14},{16,17},{19,... | collective-permute-start | bytes 2359304 | tf_op jit(solution)/shard_map/ppermute | solution.py:63
  396.4 36.1 %collective-permute-start.58 = (f32[7680]{0:T(1024)S(1)}, f32[7680]{0:T(1024)S(1)}, u32[]{:S(2)}, u32[]{:S(2)}) collective-permute-start(f32[7680]{0:T(1024)S(1)} %constant_dynamic-update-slice_fusion), channel_id=1, source_target_pairs={{0,4},{4,0},{8,12},{12,8},{16,20},{20,16},{24,28},{28,24},{1,5},{5... | collective-permute-start | bytes 92168 | tf_op jit(solution)/shard_map/ppermute | solution.py:140
  402.2 30.3 %collective-permute-start.55 = (f32[1536]{0:T(1024)S(1)}, f32[1536]{0:T(1024)S(1)}, u32[]{:S(2)}, u32[]{:S(2)}) collective-permute-start(f32[1536]{0:T(1024)S(1)} %add.480), channel_id=1, source_target_pairs={{0,16},{4,20},{8,24},{12,28},{16,0},{20,4},{24,8},{28,12},{1,17},{... | collective-permute-start | bytes 18440 | tf_op jit(solution)/shard_map/ppermute | solution.py:140
  436.2 42.8 %collective-permute-start.63 = (bf16[4,2,2,96,768]{4,3,0,2,1:T(8,128)(2,1)}, bf16[4,2,2,96,768]{4,3,0,2,1:T(8,128)(2,1)S(1)}, u32[]{:S(2)}, u32[]{:S(2)}) collective-permute-start(bf16[4,2,2,96,768]{4,3,0,2,1:T(8,128)(2,1)} %bitcast.364), channel_id=1, source_target_pairs={{0,4},{4,0},{8,12},{12,8},{16,20},{20,16},{24,28},{28,24},{1,5},{5... | collective-permute-start | bytes 7077896 | tf_op jit(solution)/shard_map/ppermute | solution.py:116
  436.5 16.7 %collective-permute-start.57 = (f32[1536]{0:T(1024)S(1)}, f32[1536]{0:T(1024)S(1)}, u32[]{:S(2)}, u32[]{:S(2)}) collective-permute-start(f32[1536]{0:T(1024)S(1)} %add.482), channel_id=1, source_target_pairs={{0,2},{1,3},{2,0},{3,1},{4,6},{5,7},{6,4},{7,5},{8,10},{9,11},{10,... | collective-permute-start | bytes 18440 | tf_op jit(solution)/shard_map/ppermute | solution.py:142
  446.3 29.3 %collective-permute-start.42 = (bf16[512,768]{1,0:T(8,128)(2,1)S(1)}, bf16[512,768]{1,0:T(8,128)(2,1)S(1)}, u32[]{:S(2)}, u32[]{:S(2)}) collective-permute-start(bf16[512,768]{1,0:T(8,128)(2,1)S(1)} %get-tuple-element.104), channel_id=1, source_target_pairs={{1,0},{2,1},{3,2},{5,4},{6,5},{7,6},{9,8},{10,9},{11,10},{13,12},{... | collective-permute-start | bytes 2359304 | tf_op jit(solution)/shard_map/ppermute | solution.py:68
  447.6 28.0 %collective-permute-start.41 = (bf16[512,768]{1,0:T(8,128)(2,1)S(1)}, bf16[512,768]{1,0:T(8,128)(2,1)S(1)}, u32[]{:S(2)}, u32[]{:S(2)}) collective-permute-start(bf16[512,768]{1,0:T(8,128)(2,1)S(1)} %get-tuple-element.103), channel_id=1, source_target_pairs={{0,1},{1,2},{2,3},{4,5},{5,6},{6,7},{8,9},{9,10},{10,11},{12,13},{... | collective-permute-start | bytes 2359304 | tf_op jit(solution)/shard_map/ppermute | solution.py:67
  453.3 16.2 %collective-permute-start.61 = (f32[7680]{0:T(1024)S(1)}, f32[7680]{0:T(1024)S(1)}, u32[]{:S(2)}, u32[]{:S(2)}) collective-permute-start(f32[7680]{0:T(1024)S(1)} %add.486), channel_id=1, source_target_pairs={{0,1},{1,0},{2,3},{3,2},{4,5},{5,4},{6,7},{7,6},{8,9},{9,8},{10,11... | collective-permute-start | bytes 92168 | tf_op jit(solution)/shard_map/ppermute | solution.py:142
  478.3 16.2 %collective-permute-start.44 = (bf16[2,2,96,768]{3,2,0,1:T(8,128)(2,1)S(1)}, bf16[2,2,96,768]{3,2,0,1:T(8,128)(2,1)S(1)}, u32[]{:S(2)}, u32[]{:S(2)}) collective-permute-start(bf16[2,2,96,768]{3,2,0,1:T(8,128)(2,1)S(1)} %dynamic-slice_bitcast_fusion.5), channel_id=1, source_target_pairs={{0,8},{4,12},{8,0},{12,4},{16,24},{20,28},{24,16},{28,20},{1,9},{5... | collective-permute-start | bytes 1769480 | tf_op jit(solution)/shard_map/ppermute | solution.py:116
  478.4 16.7 %collective-permute-start.46 = (bf16[2,2,96,768]{3,2,0,1:T(8,128)(2,1)S(1)}, bf16[2,2,96,768]{3,2,0,1:T(8,128)(2,1)S(1)}, u32[]{:S(2)}, u32[]{:S(2)}) collective-permute-start(bf16[2,2,96,768]{3,2,0,1:T(8,128)(2,1)S(1)} %dynamic-slice_bitcast_fusion.4), channel_id=1, source_target_pairs={{0,16},{4,20},{8,24},{12,28},{16,0},{20,4},{24,8},{28,12},{1,17},{... | collective-permute-start | bytes 1769480 | tf_op jit(solution)/shard_map/ppermute | solution.py:116
  480.0 27.1 %collective-permute-start.64 = (bf16[2,2,96,768]{3,2,0,1:T(8,128)(2,1)S(1)}, bf16[2,2,96,768]{3,2,0,1:T(8,128)(2,1)S(1)}, u32[]{:S(2)}, u32[]{:S(2)}) collective-permute-start(bf16[2,2,96,768]{3,2,0,1:T(8,128)(2,1)S(1)} %dynamic-slice_bitcast_fusion.3), channel_id=1, source_target_pairs={{0,8},{4,12},{8,0},{12,4},{16,24},{20,28},{24,16},{28,20},{1,9},{5... | collective-permute-start | bytes 1769480 | tf_op jit(solution)/shard_map/ppermute | solution.py:116
  482.1 25.3 %collective-permute-start.66 = (bf16[2,2,96,768]{3,2,0,1:T(8,128)(2,1)S(1)}, bf16[2,2,96,768]{3,2,0,1:T(8,128)(2,1)S(1)}, u32[]{:S(2)}, u32[]{:S(2)}) collective-permute-start(bf16[2,2,96,768]{3,2,0,1:T(8,128)(2,1)S(1)} %dynamic-slice_bitcast_fusion.2), channel_id=1, source_target_pairs={{0,16},{4,20},{8,24},{12,28},{16,0},{20,4},{24,8},{28,12},{1,17},{... | collective-permute-start | bytes 1769480 | tf_op jit(solution)/shard_map/ppermute | solution.py:116
  484.7 35.1 %collective-permute-start.74 = (bf16[2,2,96,768]{3,2,0,1:T(8,128)(2,1)S(1)}, bf16[2,2,96,768]{3,2,0,1:T(8,128)(2,1)S(1)}, u32[]{:S(2)}, u32[]{:S(2)}) collective-permute-start(bf16[2,2,96,768]{3,2,0,1:T(8,128)(2,1)S(1)} %dynamic-slice_bitcast_fusion.1), channel_id=1, source_target_pairs={{0,8},{4,12},{8,0},{12,4},{16,24},{20,28},{24,16},{28,20},{1,9},{5... | collective-permute-start | bytes 1769480 | tf_op jit(solution)/shard_map/ppermute | solution.py:116
  494.5 25.6 %collective-permute-start.76 = (bf16[2,2,96,768]{3,2,0,1:T(8,128)(2,1)S(1)}, bf16[2,2,96,768]{3,2,0,1:T(8,128)(2,1)S(1)}, u32[]{:S(2)}, u32[]{:S(2)}) collective-permute-start(bf16[2,2,96,768]{3,2,0,1:T(8,128)(2,1)S(1)} %dynamic-slice_bitcast_fusion), channel_id=1, source_target_pairs={{0,16},{4,20},{8,24},{12,28},{16,0},{20,4},{24,8},{28,12},{1,17},{... | collective-permute-start | bytes 1769480 | tf_op jit(solution)/shard_map/ppermute | solution.py:116
  495.2 31.0 %collective-permute-start.45 = (bf16[2,96,768]{2,1,0:T(8,128)(2,1)S(1)}, bf16[2,96,768]{2,1,0:T(8,128)(2,1)S(1)}, u32[]{:S(2)}, u32[]{:S(2)}) collective-permute-start(bf16[2,96,768]{2,1,0:T(8,128)(2,1)S(1)} %dynamic-slice_bitcast_fusion.11), channel_id=1, source_target_pairs={{0,16},{4,20},{8,24},{12,28},{16,0},{20,4},{24,8},{28,12},{1,17},{... | collective-permute-start | bytes 884744 | tf_op jit(solution)/shard_map/ppermute | solution.py:116
  507.1 21.2 %collective-permute-start.47 = (bf16[2,96,768]{2,1,0:T(8,128)(2,1)S(1)}, bf16[2,96,768]{2,1,0:T(8,128)(2,1)S(1)}, u32[]{:S(2)}, u32[]{:S(2)}) collective-permute-start(bf16[2,96,768]{2,1,0:T(8,128)(2,1)S(1)} %dynamic-slice_bitcast_fusion.10), channel_id=1, source_target_pairs={{0,8},{4,12},{8,0},{12,4},{16,24},{20,28},{24,16},{28,20},{1,9},{5... | collective-permute-start | bytes 884744 | tf_op jit(solution)/shard_map/ppermute | solution.py:116
  507.4 25.8 %collective-permute-start.65 = (bf16[2,96,768]{2,1,0:T(8,128)(2,1)S(1)}, bf16[2,96,768]{2,1,0:T(8,128)(2,1)S(1)}, u32[]{:S(2)}, u32[]{:S(2)}) collective-permute-start(bf16[2,96,768]{2,1,0:T(8,128)(2,1)S(1)} %dynamic-slice_bitcast_fusion.9), channel_id=1, source_target_pairs={{0,16},{4,20},{8,24},{12,28},{16,0},{20,4},{24,8},{28,12},{1,17},{... | collective-permute-start | bytes 884744 | tf_op jit(solution)/shard_map/ppermute | solution.py:116
  520.0 18.4 %collective-permute-start.75 = (bf16[2,96,768]{2,1,0:T(8,128)(2,1)S(1)}, bf16[2,96,768]{2,1,0:T(8,128)(2,1)S(1)}, u32[]{:S(2)}, u32[]{:S(2)}) collective-permute-start(bf16[2,96,768]{2,1,0:T(8,128)(2,1)S(1)} %dynamic-slice_bitcast_fusion.7), channel_id=1, source_target_pairs={{0,16},{4,20},{8,24},{12,28},{16,0},{20,4},{24,8},{28,12},{1,17},{... | collective-permute-start | bytes 884744 | tf_op jit(solution)/shard_map/ppermute | solution.py:116
  552.6 14.6 %collective-permute-start.79 = (bf16[96,768]{1,0:T(8,128)(2,1)S(1)}, bf16[96,768]{1,0:T(8,128)(2,1)S(1)}, u32[]{:S(2)}, u32[]{:S(2)}) collective-permute-start(bf16[96,768]{1,0:T(8,128)(2,1)S(1)} %fusion.67), channel_id=1, source_target_pairs={{0,1},{3,2},{4,5},{7,6},{8,9},{11,10},{12,13},{15,14},{16,17},{19,... | collective-permute-start | bytes 442376 | tf_op jit(solution)/shard_map/ppermute | solution.py:63
  556.6 16.6 %collective-permute-start.51 = (bf16[4,96,192]{2,1,0:T(8,128)(2,1)S(1)}, bf16[4,96,192]{2,1,0:T(8,128)(2,1)S(1)}, u32[]{:S(2)}, u32[]{:S(2)}) collective-permute-start(bf16[4,96,192]{2,1,0:T(8,128)(2,1)S(1)} %get-tuple-element.136), channel_id=1, source_target_pairs={{0,1},{1,2},{2,3},{4,5},{5,6},{6,7},{8,9},{9,10},{10,11},{12,13},{... | collective-permute-start | bytes 442376 | tf_op jit(solution)/shard_map/ppermute | solution.py:67
  (108 other events, 1188.7 us)
